TPU v7x, 32 devices: a whole 2x2x4 slice. The times are simulated.
32 devices in a mesh: dp: 16 (over z, y, x), tensor: 2 (over core).
Axes of the slice: x: 2, y: 2, z: 4, core: 2. Of those that a mesh axis runs over, the one named last changes fastest.
Arguments:
- image_tokens: bfloat16 [16, 256, 1536], P('dp'), may hold values from -6 to 6
- text_tokens: bfloat16 [16, 154, 1536], P('dp'), may hold values from -6 to 6
- image_cotangent: bfloat16 [16, 256, 1536], P('dp'), may hold values from -6 to 6
- text_cotangent: bfloat16 [16, 154, 1536], P('dp'), may hold values from -6 to 6
- timesteps: int32 [16], replicated, may hold values from 0 to 999
- mod_weight: float32 [2, 1536, 9216], P(None, None, ('dp', 'tensor')), may hold values from -0.15625 to 0.15625
- mod_bias: float32 [2, 9216], P(None, ('dp', 'tensor')), may hold values from -0.5 to 0.5
- qkv_weight: float32 [2, 1536, 3, 1536], P(None, 'dp', None, 'tensor'), may hold values from -1.2247449 to 1.2247449
- proj_weight: float32 [2, 1536, 1536], P(None, 'tensor', 'dp'), may hold values from -0.625 to 0.625
- up_weight: float32 [2, 1536, 6144], P(None, 'dp', 'tensor'), may hold values from -0.15625 to 0.15625
- down_weight: float32 [2, 6144, 1536], P(None, 'tensor', 'dp'), may hold values from -0.078125 to 0.078125
- mean_mod: float32 [2, 1536, 9216], P(None, None, ('dp', 'tensor')), may hold values from -3 to 3
- second_mod: float32 [2, 1536, 9216], P(None, None, ('dp', 'tensor')), may hold values from 0.01 to 0.5
- mean_bias: float32 [2, 9216], P(None, ('dp', 'tensor')), may hold values from -3 to 3
- second_bias: float32 [2, 9216], P(None, ('dp', 'tensor')), may hold values from 0.01 to 0.5
- mean_qkv: float32 [2, 1536, 3, 1536], P(None, 'dp', None, 'tensor'), may hold values from -3 to 3
- second_qkv: float32 [2, 1536, 3, 1536], P(None, 'dp', None, 'tensor'), may hold values from 0.01 to 0.5
- mean_proj: float32 [2, 1536, 1536], P(None, 'tensor', 'dp'), may hold values from -3 to 3
- second_proj: float32 [2, 1536, 1536], P(None, 'tensor', 'dp'), may hold values from 0.01 to 0.5
- mean_up: float32 [2, 1536, 6144], P(None, 'dp', 'tensor'), may hold values from -3 to 3
- second_up: float32 [2, 1536, 6144], P(None, 'dp', 'tensor'), may hold values from 0.01 to 0.5
- mean_down: float32 [2, 6144, 1536], P(None, 'tensor', 'dp'), may hold values from -3 to 3
- second_down: float32 [2, 6144, 1536], P(None, 'tensor', 'dp'), may hold values from 0.01 to 0.5
Outputs:
- image_out: float32 [16, 256, 1536], P('dp')
- text_out: float32 [16, 154, 1536], P('dp')
- image_grad: float32 [16, 256, 1536], P('dp')
- text_grad: float32 [16, 154, 1536], P('dp')
- grad_mod: float32 [2, 1536, 9216], P(None, None, ('dp', 'tensor'))
- grad_bias: float32 [2, 9216], P(None, ('dp', 'tensor'))
- grad_qkv: float32 [2, 1536, 3, 1536], P(None, 'dp', None, 'tensor')
- grad_proj: float32 [2, 1536, 1536], P(None, 'tensor', 'dp')
- grad_up: float32 [2, 1536, 6144], P(None, 'dp', 'tensor')
- grad_down: float32 [2, 6144, 1536], P(None, 'tensor', 'dp')
- new_mod: float32 [2, 1536, 9216], P(None, None, ('dp', 'tensor'))
- new_bias: float32 [2, 9216], P(None, ('dp', 'tensor'))
- new_qkv: float32 [2, 1536, 3, 1536], P(None, 'dp', None, 'tensor')
- new_proj: float32 [2, 1536, 1536], P(None, 'tensor', 'dp')
- new_up: float32 [2, 1536, 6144], P(None, 'dp', 'tensor')
- new_down: float32 [2, 6144, 1536], P(None, 'tensor', 'dp')
- mean_mod_next: float32 [2, 1536, 9216], P(None, None, ('dp', 'tensor'))
- second_mod_next: float32 [2, 1536, 9216], P(None, None, ('dp', 'tensor'))
- mean_bias_next: float32 [2, 9216], P(None, ('dp', 'tensor'))
- second_bias_next: float32 [2, 9216], P(None, ('dp', 'tensor'))
- mean_qkv_next: float32 [2, 1536, 3, 1536], P(None, 'dp', None, 'tensor')
- second_qkv_next: float32 [2, 1536, 3, 1536], P(None, 'dp', None, 'tensor')
- mean_proj_next: float32 [2, 1536, 1536], P(None, 'tensor', 'dp')
- second_proj_next: float32 [2, 1536, 1536], P(None, 'tensor', 'dp')
- mean_up_next: float32 [2, 1536, 6144], P(None, 'dp', 'tensor')
- second_up_next: float32 [2, 1536, 6144], P(None, 'dp', 'tensor')
- mean_down_next: float32 [2, 6144, 1536], P(None, 'tensor', 'dp')
- second_down_next: float32 [2, 6144, 1536], P(None, 'tensor', 'dp')
All inputs are finite; a program needn't handle non-finite values.
Results may differ from a plain program's by a relative error of at most 0.012.
Values may be sent and summed in bfloat16 or wider, within the bound.
No kernel may reach another device: no remote copies, remote signals or barrier semaphores. Data moves between devices by JAX's collectives and lax.ppermute only.
A program may use at most 384 MiB of HBM per device.

v0:
```python
import functools
import math

import jax
import jax.numpy as jnp
from jax import lax
from jax.experimental import pallas as pl
from jax.experimental.pallas import tpu as pltpu
from jax.sharding import Mesh
from jax.sharding import PartitionSpec as P


HD = 64
ADAM_STEP = 10
INNER = 4

eps_norm = 1e-06
beta_one = 0.9
beta_two = 0.999
adam_eps = 1e-08
learn_rate = 0.02
decay_rate = 0.1
gelu_coef = 0.7978845608028654
cubic_coef = 0.044715
score_scale = 1.0 / math.sqrt(HD)
NEGATIVE = -1e30
LANES = 128
CHUNK = 16

F32 = jnp.float32
BF16 = jnp.bfloat16


def layer_norm(values):
    average = jnp.mean(values, axis=-1, keepdims=True)
    centred = values - average
    variance = jnp.mean(centred * centred, axis=-1, keepdims=True)
    inv_std = lax.rsqrt(variance + eps_norm)
    return (centred * inv_std, inv_std)


def norm_back(grad_normed, normed, inv_std):
    mean_grad = jnp.mean(grad_normed, axis=-1, keepdims=True)
    mean_cross = jnp.mean(grad_normed * normed, axis=-1, keepdims=True)
    return inv_std * (grad_normed - mean_grad - normed * mean_cross)


def gelu_pair(inputs):
    argument = gelu_coef * (inputs + cubic_coef * inputs * inputs * inputs)
    tangent = jnp.tanh(argument)
    activated = 0.5 * inputs * (1.0 + tangent)
    derivative = 0.5 * (1.0 + tangent) + 0.5 * inputs * (1.0 - tangent * tangent) * gelu_coef * (
        1.0 + 3.0 * cubic_coef * inputs * inputs
    )
    return (activated, derivative)


def adam_step(weight, gradient, mean_old, second_old):
    mean_new = beta_one * mean_old + (1.0 - beta_one) * gradient
    second_new = beta_two * second_old + (1.0 - beta_two) * gradient * gradient
    mean_hat = mean_new / (1.0 - beta_one**ADAM_STEP)
    second_hat = second_new / (1.0 - beta_two**ADAM_STEP)
    updated = weight - learn_rate * (
        mean_hat / (jnp.sqrt(second_hat) + adam_eps) + decay_rate * weight
    )
    return (updated, mean_new, second_new)


def dot_nn(a, b):
    return lax.dot_general(a, b, (((1,), (0,)), ((), ())), preferred_element_type=F32)


def dot_nt(a, b):
    return lax.dot_general(a, b, (((1,), (1,)), ((), ())), preferred_element_type=F32)


def dot_tn(a, b):
    return lax.dot_general(a, b, (((0,), (0,)), ((), ())), preferred_element_type=F32)


def key_bias(valid_ref, rows, padded):
    image, text = rows
    column = lax.broadcasted_iota(jnp.int32, (1, padded), 1)
    first = 2 * image
    second = first + text
    real = (column < first + valid_ref[0]) | ((column >= second) & (column < second + valid_ref[1]))
    return jnp.where(real, 0.0, NEGATIVE)


def pieces_of(rows):
    image, text = rows
    return ((0, image), (image, image), (2 * image, text), (2 * image + text, text))


def attend_kernel(rows, heads, padded, valid_ref, *refs):
    qkv, contexts, lse_ref, joint = (refs[:4], refs[4:8], refs[8], refs[9])
    width = heads * HD
    pieces = pieces_of(rows)
    total = 2 * sum(rows)
    for ref, (offset, size) in zip(qkv, pieces):
        joint[offset : offset + size, :] = ref[:, : 3 * width]
    if padded > total:
        joint[total:, :] = jnp.zeros((padded - total, 3 * width), BF16)
    bias = key_bias(valid_ref, rows, padded)
    for out in contexts:
        out[:, : 3 * width] = jnp.zeros((out.shape[0], 3 * width), BF16)
    for head in range(heads):
        at = head * HD
        keys = joint[:, width + at : width + at + HD]
        values = joint[:, 2 * width + at : 2 * width + at + HD]
        for ref, out, (offset, size) in zip(qkv, contexts, pieces):
            scores = dot_nt(ref[:, at : at + HD], keys) * score_scale + bias
            highest = jnp.max(scores, axis=-1, keepdims=True)
            weights = jnp.exp(scores - highest)
            totals = jnp.sum(weights, axis=-1, keepdims=True)
            probs = (weights * (1.0 / totals)).astype(BF16)
            out[:, 3 * width + at : 3 * width + at + HD] = dot_nn(probs, values).astype(BF16)
            lse_ref[offset : offset + size, head : head + 1] = highest + jnp.log(totals)


def attend_back_kernel(rows, heads, padded, valid_ref, *refs):
    qkv, contexts, grads, lse_ref = (refs[:4], refs[4:8], refs[8:12], refs[12])
    outs, joint, key_sum, value_sum = (refs[13:17], refs[17], refs[18], refs[19])
    width = heads * HD
    pieces = pieces_of(rows)
    total = 2 * sum(rows)
    for ref, (offset, size) in zip(qkv, pieces):
        joint[offset : offset + size, :] = ref[:, : 3 * width]
    if padded > total:
        joint[total:, :] = jnp.zeros((padded - total, 3 * width), BF16)
    for out in outs:
        out[:, 3 * width :] = jnp.zeros((out.shape[0], width), BF16)
    bias = key_bias(valid_ref, rows, padded)
    for head in range(heads):
        at = head * HD
        keys = joint[:, width + at : width + at + HD]
        values = joint[:, 2 * width + at : 2 * width + at + HD]
        for number, (offset, size) in enumerate(pieces):
            queries = qkv[number][:, at : at + HD]
            grad_context = grads[number][:, 3 * width + at : 3 * width + at + HD]
            context = contexts[number][:, 3 * width + at : 3 * width + at + HD]
            scores = dot_nt(queries, keys) * score_scale + bias
            probs = jnp.exp(scores - lse_ref[offset : offset + size, head : head + 1])
            grad_probs = dot_nt(grad_context, values)
            row_dots = jnp.sum(
                grad_context.astype(F32) * context.astype(F32), axis=-1, keepdims=True
            )
            grad_scores = (probs * (grad_probs - row_dots) * score_scale).astype(BF16)
            outs[number][:, at : at + HD] = dot_nn(grad_scores, keys).astype(BF16)
            value_part = dot_tn(probs.astype(BF16), grad_context)
            key_part = dot_tn(grad_scores, queries)
            if number == 0:
                value_sum[...] = value_part
                key_sum[...] = key_part
            else:
                value_sum[...] += value_part
                key_sum[...] += key_part
        for number, (offset, size) in enumerate(pieces):
            outs[number][:, width + at : width + at + HD] = key_sum[
                offset : offset + size, :
            ].astype(BF16)
            outs[number][:, 2 * width + at : 2 * width + at + HD] = value_sum[
                offset : offset + size, :
            ].astype(BF16)


def piece_specs(rows, columns):
    image, text = rows
    return [pl.BlockSpec((size, columns), lambda s, v: (s, 0)) for size in (image, image, text, text)]


def attend(rows, heads, seqs, valid, qkv):
    total = 2 * sum(rows)
    padded = -(-total // LANES) * LANES
    width = heads * HD
    sizes = (rows[0], rows[0], rows[1], rows[1])
    return pl.pallas_call(
        functools.partial(attend_kernel, rows, heads, padded),
        grid_spec=pltpu.PrefetchScalarGridSpec(
            num_scalar_prefetch=1,
            grid=(seqs,),
            in_specs=piece_specs(rows, qkv[0].shape[1]),
            out_specs=piece_specs(rows, 4 * width)
            + [pl.BlockSpec((None, total, LANES), lambda s, v: (s, 0, 0))],
            scratch_shapes=[pltpu.VMEM((padded, 3 * width), BF16)],
        ),
        out_shape=[jax.ShapeDtypeStruct((seqs * size, 4 * width), BF16) for size in sizes]
        + [jax.ShapeDtypeStruct((seqs, total, LANES), F32)],
        cost_estimate=pl.CostEstimate(
            flops=4 * seqs * heads * total * total * HD,
            bytes_accessed=8 * seqs * total * width,
            transcendentals=seqs * heads * total * total,
        ),
        name="attend",
    )(valid, *qkv)


def attend_back(rows, heads, seqs, valid, qkv, contexts, grads, lse):
    total = 2 * sum(rows)
    padded = -(-total // LANES) * LANES
    width = heads * HD
    sizes = (rows[0], rows[0], rows[1], rows[1])
    return pl.pallas_call(
        functools.partial(attend_back_kernel, rows, heads, padded),
        grid_spec=pltpu.PrefetchScalarGridSpec(
            num_scalar_prefetch=1,
            grid=(seqs,),
            in_specs=piece_specs(rows, qkv[0].shape[1])
            + piece_specs(rows, 4 * width)
            + piece_specs(rows, 4 * width)
            + [pl.BlockSpec((None, total, LANES), lambda s, v: (s, 0, 0))],
            out_specs=piece_specs(rows, 4 * width),
            scratch_shapes=[
                pltpu.VMEM((padded, 3 * width), BF16),
                pltpu.VMEM((padded, HD), F32),
                pltpu.VMEM((padded, HD), F32),
            ],
        ),
        out_shape=[jax.ShapeDtypeStruct((seqs * size, 4 * width), BF16) for size in sizes],
        cost_estimate=pl.CostEstimate(
            flops=10 * seqs * heads * total * total * HD,
            bytes_accessed=20 * seqs * total * width,
            transcendentals=seqs * heads * total * total,
        ),
        name="attend_back",
    )(valid, *qkv, *contexts, *grads, lse)


def swap_core(values):
    return lax.ppermute(values, "tensor", [(0, 1), (1, 0)])


def hop(values, distance, count):
    return lax.ppermute(values, "inner", [(i, i ^ distance) for i in range(count)])


def start_rows(rows, count):
    return [rows] + [hop(rows, j, count) for j in range(1, count)]


def finish_rows(blocks):
    own = jnp.concatenate(blocks, axis=0)
    return (own, swap_core(own))


def gather_rows(rows, count):
    return finish_rows(start_rows(rows, count))


def finish_both(blocks, image):
    return [
        finish_rows([block[part] for block in blocks])
        for part in (slice(image), slice(image, None))
    ]


def send_rows(own, other, count):
    arrived = swap_core(other.astype(BF16))
    blocks = (own + arrived.astype(F32)).reshape(count, own.shape[0] // count, own.shape[1])
    low = blocks.astype(BF16)
    return (blocks[0], [hop(low[j], j, count) for j in range(1, count)])


def add_rows(sent):
    total, parts = sent
    for part in parts:
        total = total + part.astype(F32)
    return total


def send_both(partials, count):
    arrived = swap_core(jnp.concatenate([p[1].astype(BF16) for p in partials], axis=0))
    middle = partials[0][0].shape[0]
    sums = [
        (p[0] + part.astype(F32)).reshape(count, p[0].shape[0] // count, p[0].shape[1])
        for p, part in zip(partials, (arrived[:middle], arrived[middle:]))
    ]
    lows = [
        jnp.concatenate([part[j].astype(BF16) for part in sums], axis=0)
        for j in range(1, count)
    ]
    return ([part[0] for part in sums], [hop(lows[j - 1], j, count) for j in range(1, count)])


def by_place(me_ref, count, body):
    for number in range(count):
        pl.when(me_ref[0] == number)(functools.partial(body, number))


def pack_attn_kernel(count, me_ref, qkv_ref, proj_ref, *outs):
    columns = proj_ref.shape[2] // count

    def place(number):
        for j, out in enumerate(outs):
            at = (j ^ number) * columns
            for n in range(2):
                base = 4 * n * columns
                for k in range(3):
                    out[:, base + k * columns : base + (k + 1) * columns] = qkv_ref[
                        n, k, :, at : at + columns
                    ].astype(BF16)
                out[:, base + 3 * columns : base + 4 * columns] = proj_ref[
                    n, :, at : at + columns
                ].astype(BF16)

    by_place(me_ref, count, place)


def pack_attn(me, qkv, proj, count):
    slab, full = proj.shape[1:]
    shape = jax.ShapeDtypeStruct((slab, 8 * full // count), BF16)
    return pl.pallas_call(
        functools.partial(pack_attn_kernel, count),
        grid_spec=pltpu.PrefetchScalarGridSpec(
            num_scalar_prefetch=1,
            grid=(1,),
            in_specs=[
                pl.BlockSpec(qkv.shape, lambda i, m: (0, 0, 0, 0)),
                pl.BlockSpec(proj.shape, lambda i, m: (0, 0, 0)),
            ],
            out_specs=[pl.BlockSpec(shape.shape, lambda i, m: (0, 0))] * count,
        ),
        out_shape=[shape] * count,
    )(me, qkv, proj)


def pack_ff_kernel(count, me_ref, up_ref, down_ref, *outs):
    columns = up_ref.shape[1] // count

    def place(number):
        for j, out in enumerate(outs):
            at = (j ^ number) * columns
            out[:, :columns] = up_ref[:, at : at + columns].astype(BF16)
            out[:, columns:] = down_ref[:, at : at + columns].astype(BF16)

    by_place(me_ref, count, place)


def pack_ff(me, up, down, n, count):
    slab, full = up.shape[1:]
    shape = jax.ShapeDtypeStruct((slab, 2 * full // count), BF16)
    spec = pl.BlockSpec((None, slab, full), lambda i, m: (n, 0, 0))
    return pl.pallas_call(
        functools.partial(pack_ff_kernel, count),
        grid_spec=pltpu.PrefetchScalarGridSpec(
            num_scalar_prefetch=1,
            grid=(1,),
            in_specs=[spec, spec],
            out_specs=[pl.BlockSpec(shape.shape, lambda i, m: (0, 0))] * count,
        ),
        out_shape=[shape] * count,
    )(me, up, down)


def unpack_kernel(count, me_ref, *refs):
    blocks, out = (refs[:count], refs[count])
    slab = blocks[0].shape[0]

    def place(number):
        for j, block in enumerate(blocks):
            at = (j ^ number) * slab
            out[at : at + slab, :] = block[...]

    by_place(me_ref, count, place)


def unpack(me, blocks):
    count = len(blocks)
    slab, columns = blocks[0].shape
    return pl.pallas_call(
        functools.partial(unpack_kernel, count),
        grid_spec=pltpu.PrefetchScalarGridSpec(
            num_scalar_prefetch=1,
            grid=(1,),
            in_specs=[pl.BlockSpec((slab, columns), lambda i, m: (0, 0))] * count,
            out_specs=pl.BlockSpec((count * slab, columns), lambda i, m: (0, 0)),
        ),
        out_shape=jax.ShapeDtypeStruct((count * slab, columns), BF16),
    )(me, *blocks)


def adam_refs(gradient, weight, mean, second, outs):
    updated, mean_new, second_new = adam_step(weight, gradient, mean, second)
    for out, value in zip(outs, (gradient, updated, mean_new, second_new)):
        out[...] = value


def adam_ff_kernel(count, me_ref, *refs):
    blocks, (weight, mean, second) = (refs[:count], refs[count : count + 3])
    outs, gradient = (refs[-5:-1], refs[-1])
    wanted = pl.program_id(0) ^ me_ref[0]
    for j, block in enumerate(blocks):

        @pl.when(wanted == j)
        def take(block=block):
            gradient[...] = block[...].astype(F32)

    adam_refs(gradient[...], weight[...], mean[...], second[...], outs)


def adam_ff(me, blocks, half, weight, mean, second, n, before):
    count = len(blocks)
    slab, columns = (blocks[0].shape[0], blocks[0].shape[1] // 2)
    spec = pl.BlockSpec((None, slab, columns), lambda c, m: (n, 0, c))
    return pl.pallas_call(
        functools.partial(adam_ff_kernel, count),
        grid_spec=pltpu.PrefetchScalarGridSpec(
            num_scalar_prefetch=1,
            grid=(count,),
            in_specs=[pl.BlockSpec((slab, columns), lambda c, m: (0, half))] * count
            + [spec] * 3
            + [pl.BlockSpec(memory_space=pl.ANY)] * len(before),
            out_specs=[spec] * 4,
            scratch_shapes=[pltpu.VMEM((slab, columns), F32)],
        ),
        out_shape=[jax.ShapeDtypeStruct(weight.shape, F32)] * 4,
        input_output_aliases={1 + count + 3 + i: i for i in range(len(before))},
    )(me, *blocks, weight, mean, second, *before)


def adam_attn_kernel(count, me_ref, *refs):
    blocks, weights = (refs[:count], refs[count : count + 6])
    qkv_outs, proj_outs = (refs[-10:-6], refs[-6:-2])
    qkv_grad, proj_grad = refs[-2:]
    columns = proj_grad.shape[1] // count

    def place(number):
        for j, block in enumerate(blocks):
            at = (j ^ number) * columns
            for k in range(3):
                qkv_grad[k, :, at : at + columns] = block[
                    :, k * columns : (k + 1) * columns
                ].astype(F32)
            proj_grad[:, at : at + columns] = block[:, 3 * columns :].astype(F32)

    by_place(me_ref, count, place)
    adam_refs(qkv_grad[...], weights[0][...], weights[1][...], weights[2][...], qkv_outs)
    adam_refs(proj_grad[...], weights[3][...], weights[4][...], weights[5][...], proj_outs)


def adam_attn(me, blocks, qkv, proj, n, before):
    count = len(blocks)
    slab, full = proj[0].shape[1:]
    qkv_spec = pl.BlockSpec((None, 3, slab, full), lambda i, m: (n, 0, 0, 0))
    proj_spec = pl.BlockSpec((None, slab, full), lambda i, m: (n, 0, 0))
    return pl.pallas_call(
        functools.partial(adam_attn_kernel, count),
        grid_spec=pltpu.PrefetchScalarGridSpec(
            num_scalar_prefetch=1,
            grid=(1,),
            in_specs=[pl.BlockSpec(blocks[0].shape, lambda i, m: (0, 0))] * count
            + [qkv_spec] * 3
            + [proj_spec] * 3
            + [pl.BlockSpec(memory_space=pl.ANY)] * len(before),
            out_specs=[qkv_spec] * 4 + [proj_spec] * 4,
            scratch_shapes=[pltpu.VMEM((3, slab, full), F32), pltpu.VMEM((slab, full), F32)],
        ),
        out_shape=[jax.ShapeDtypeStruct(qkv[0].shape, F32)] * 4
        + [jax.ShapeDtypeStruct(proj[0].shape, F32)] * 4,
        input_output_aliases={1 + count + 6 + i: i for i in range(len(before))},
    )(me, *blocks, *qkv, *proj, *before)


def exchange(blocks, count):
    return [blocks[0]] + [hop(blocks[j], j, count) for j in range(1, count)]


def after(values, *done):
    return jax.tree.map(lambda value: lax.optimization_barrier((value, done))[0], values)


def whole(array):
    return pl.BlockSpec(array.shape, lambda i, m: (0,) * len(array.shape))


def row_kernel(body, place, inputs, outputs, scratch=()):
    return pl.pallas_call(
        body,
        grid_spec=pltpu.PrefetchScalarGridSpec(
            num_scalar_prefetch=1,
            grid=(1,),
            in_specs=[whole(a) for a in inputs],
            out_specs=[whole(a) for a in outputs],
            scratch_shapes=list(scratch),
        ),
        out_shape=list(outputs),
    )(place, *inputs)


def fold(values):
    return jnp.sum(values.reshape(values.shape[0] // 8, 8, values.shape[1]), axis=0)


def arrived_rows(own, parts, where, offset):
    total = own[where, :]
    for part in parts:
        total = total + part[pl.ds(pl.multiple_of(offset, CHUNK), CHUNK), :].astype(F32)
    return total


def middle_back_kernel(n, me_ref, own, *refs):
    parts, (middle, attn, cotangent, mods) = (refs[:-7], refs[-7:-3])
    grad_out, low_out, sums_out = refs[-3:]
    zero = jnp.zeros((8, own.shape[1]), F32)
    scale, gate = (mods[n, 4:5, :], mods[n, 2:3, :])

    def step(i, sums):
        where = pl.ds(pl.multiple_of(i * CHUNK, CHUNK), CHUNK)
        grad = arrived_rows(own, parts, where, i * CHUNK)
        normed, inv_std = layer_norm(middle[where, :])
        total = cotangent[where, :].astype(F32) + norm_back(grad * (1.0 + scale), normed, inv_std)
        grad_out[where, :] = total
        low_out[where, :] = (total * gate).astype(BF16)
        terms = (total * attn[where, :], grad, grad * normed)
        return tuple(a + fold(b) for a, b in zip(sums, terms))

    sums = lax.fori_loop(0, own.shape[0] // CHUNK, step, (zero,) * 3)
    for k, value in enumerate(sums):
        sums_out[k : k + 1, :] = jnp.sum(value, axis=0, keepdims=True)


def middle_back(place, n, sent, middle, attn, cotangent, mods):
    own, parts = sent
    return row_kernel(
        functools.partial(middle_back_kernel, n),
        place,
        (own, *parts, middle, attn, cotangent, mods),
        (
            jax.ShapeDtypeStruct(own.shape, F32),
            jax.ShapeDtypeStruct(own.shape, BF16),
            jax.ShapeDtypeStruct((8, own.shape[1]), F32),
        ),
    )


def end_kernel(arrivals, me_ref, *refs):
    mods, back = (refs[0], refs[1 : 1 + arrivals])
    streams = refs[1 + arrivals : -4]
    each = len(streams) // 2
    grads_out, rows_out, owners_out, table = refs[-4:]
    offset = 0
    for n in range(2):
        own, tokens, grad_middle, cotangent, middle, sums, down = streams[n * each :][:7]
        parts = streams[n * each + 7 : (n + 1) * each]
        zero = jnp.zeros((8, own.shape[1]), F32)
        scale, gate = (mods[n, 1:2, :], mods[n, 5:6, :])

        def step(i, totals):
            where = pl.ds(pl.multiple_of(i * CHUNK, CHUNK), CHUNK)
            place = pl.ds(pl.multiple_of(offset + i * CHUNK, CHUNK), CHUNK)
            grad = arrived_rows(own, back, where, offset + i * CHUNK)
            normed, inv_std = layer_norm(tokens[where, :].astype(F32))
            grads_out[place, :] = grad_middle[where, :] + norm_back(
                grad * (1.0 + scale), normed, inv_std
            )
            total = arrived_rows(down, parts, where, i * CHUNK)
            rows_out[place, :] = middle[where, :] + gate * total
            terms = (grad, grad * normed, cotangent[where, :].astype(F32) * total)
            return tuple(a + fold(b) for a, b in zip(totals, terms))

        totals = lax.fori_loop(0, own.shape[0] // CHUNK, step, (zero,) * 3)
        for k, value in zip((0, 1, 5), totals):
            table[6 * n + k : 6 * n + k + 1, :] = jnp.sum(value, axis=0, keepdims=True)
        table[6 * n + 2 : 6 * n + 5, :] = sums[0:3, :]
        offset += own.shape[0]
    width = table.shape[1]
    devices, _, columns = owners_out.shape
    for n in range(2):
        for d in range(devices):
            done = 0
            while done < columns:
                k, at = divmod(d * columns + done, width)
                size = min(columns - done, width - at)
                owners_out[d, n : n + 1, done : done + size] = table[
                    6 * n + k : 6 * n + k + 1, at : at + size
                ]
                done += size


def end_rows(place, mods, sent_one, streams, down_sent, devices):
    owns, back = sent_one
    inputs = [mods, *back]
    for n in range(2):
        inputs += [owns[n], *streams[n], down_sent[n][0], *down_sent[n][1]]
    rows, width = back[0].shape
    columns = 6 * width // devices
    return row_kernel(
        functools.partial(end_kernel, len(back)),
        place,
        inputs,
        (
            jax.ShapeDtypeStruct((rows, width), F32),
            jax.ShapeDtypeStruct((rows, width), F32),
            jax.ShapeDtypeStruct((devices, 2, columns), F32),
        ),
        (pltpu.VMEM((16, width), F32),),
    )


def whole_rows_kernel(core_ref, own, other, *outs):
    for core in range(2):

        @pl.when(core_ref[0] == core)
        def place(core=core):
            start = 0
            for out in outs:
                length = out.shape[1]
                size = (own.shape[0] - start) if start else length // 2
                for number, source in ((core, own), (1 - core, other)):
                    count = min(size, length - number * size)
                    out[0, number * size : number * size + count, :] = source[
                        start : start + count, :
                    ]
                start += size


def whole_rows(core, own, lengths):
    return row_kernel(
        whole_rows_kernel,
        core,
        (own, swap_core(own)),
        [jax.ShapeDtypeStruct((1, length, own.shape[1]), F32) for length in lengths],
    )


def attn_gradient_kernel(columns, me_ref, *refs):
    shifted, grads, proj_ins, contexts, out = (refs[:2], refs[2:4], refs[4:6], refs[6:8], refs[8])
    full = out.shape[1]
    split = columns // 256 * 256
    for low, high in ((0, split), (split, full)):
        total = None
        terms = list(zip(shifted, grads))
        if high > columns:
            terms += list(zip(proj_ins, contexts))
        for left, right in terms:
            part = dot_tn(left[...], right[:, low:high])
            total = part if total is None else total + part
        out[:, low:high] = total.astype(BF16)


def attn_gradient(place, columns, shifted, grads, proj_ins, contexts):
    width = shifted[0].shape[1]
    full = grads[0].shape[1]
    tile = math.gcd(512, width)
    left = [pl.BlockSpec((a.shape[0], tile), lambda i, m: (0, i)) for a in shifted]
    right = [pl.BlockSpec(a.shape, lambda i, m: (0, 0)) for a in grads]
    rows = shifted[0].shape[0]
    return pl.pallas_call(
        functools.partial(attn_gradient_kernel, columns),
        grid_spec=pltpu.PrefetchScalarGridSpec(
            num_scalar_prefetch=1,
            grid=(width // tile,),
            in_specs=(left + right) * 2,
            out_specs=pl.BlockSpec((tile, full), lambda i, m: (i, 0)),
        ),
        out_shape=jax.ShapeDtypeStruct((width, full), BF16),
        cost_estimate=pl.CostEstimate(
            flops=4 * rows * width * full, bytes_accessed=8 * rows * width, transcendentals=0
        ),
    )(place, *shifted, *grads, *proj_ins, *contexts)


def local(
    image_tokens,
    text_tokens,
    image_cotangent,
    text_cotangent,
    timesteps,
    mod_weight,
    mod_bias,
    qkv_weight,
    proj_weight,
    up_weight,
    down_weight,
    mean_mod,
    second_mod,
    mean_bias,
    second_bias,
    mean_qkv,
    second_qkv,
    mean_proj,
    second_proj,
    mean_up,
    second_up,
    mean_down,
    second_down,
):
    count = lax.axis_size("inner")
    cores = lax.axis_size("tensor")
    me = lax.axis_index("inner")
    core = lax.axis_index("tensor")
    every = ("outer", "inner", "tensor")
    streams = (0, 1)
    seq_count = timesteps.shape[0]
    devices = seq_count * cores
    column_count = mod_weight.shape[2]
    width = image_tokens.shape[2]
    slab = qkv_weight.shape[1]
    head_cols = qkv_weight.shape[3] // count
    heads = head_cols // HD
    unit_cols = up_weight.shape[2] // count
    lengths = (image_tokens.shape[1], text_tokens.shape[1])
    rows = tuple(-(-length // (16 * cores)) * 16 for length in lengths)

    place = me.astype(jnp.int32)[None]
    qkv_all = [a.transpose(0, 2, 1, 3) for a in (qkv_weight, mean_qkv, second_qkv)]
    proj_all = [a.transpose(0, 2, 1) for a in (proj_weight, mean_proj, second_proj)]
    up_all = (up_weight, mean_up, second_up)
    down_all = [a.transpose(0, 2, 1) for a in (down_weight, mean_down, second_down)]

    def full_weight(shard):
        return lax.all_gather(shard, "outer", axis=0, tiled=True)

    blocks = pack_attn(place, qkv_all[0], proj_all[0], count)
    shard = unpack(place, exchange(blocks, count))
    attn_both = full_weight(shard)

    half_width = width // 2
    frequency = jnp.exp(-math.log(10000.0) * jnp.arange(half_width, dtype=F32) / half_width)
    angles = timesteps.astype(F32)[:, None] * frequency[None, :]
    all_cond = jax.nn.silu(jnp.concatenate([jnp.cos(angles), jnp.sin(angles)], axis=1)).astype(BF16)
    bias_low = lax.optimization_barrier(mod_bias.astype(BF16)).astype(F32)
    local_mod = (
        jnp.einsum("sd,ndc->snc", all_cond, mod_weight.astype(BF16), preferred_element_type=F32)
        + bias_low[None, :, :]
    )
    to_cores = jnp.broadcast_to(
        local_mod[:, None], (seq_count, cores, 2, column_count)
    ).reshape(devices, 2, column_count)
    spread = lax.all_to_all(to_cores, every, split_axis=0, concat_axis=0, tiled=True)
    mods = after(spread, shard).transpose(1, 0, 2).reshape(2, 6, width)

    def own_rows(tokens, size):
        short = cores * size - tokens.shape[1]
        padded = jnp.pad(tokens[0], ((0, short), (0, 0)))
        return lax.dynamic_slice(padded, (core * size, 0), (size, width))

    tokens = [own_rows(t, r) for t, r in zip((image_tokens, text_tokens), rows)]
    inputs = [t.astype(F32) for t in tokens]
    cotangents = [own_rows(t, r) for t, r in zip((image_cotangent, text_cotangent), rows)]
    valid = jnp.stack(
        [
            jnp.clip(lengths[1] - core * rows[1], 0, rows[1]),
            jnp.clip(lengths[1] - (1 - core) * rows[1], 0, rows[1]),
        ]
    ).astype(jnp.int32)

    shifted_one = []
    for n in streams:
        normed, _ = layer_norm(inputs[n])
        shifted_one.append((normed * (1.0 + mods[n, 1]) + mods[n, 0]).astype(BF16))
    shifted_one = finish_both(start_rows(jnp.concatenate(shifted_one, axis=0), count), rows[0])

    def ff_blocks(n, where):
        return exchange(pack_ff(where, up_all[0], down_all[0], n, count), count)

    shard = unpack(place, ff_blocks(0, after(place, shifted_one)))
    ff_full = [full_weight(shard)]
    blocks = ff_blocks(1, after(place, shard))
    gated = [
        (after(cotangents[n], shard).astype(F32) * mods[n, 5]).astype(BF16) for n in streams
    ]
    gated = start_rows(jnp.concatenate(gated, axis=0), count)

    wide = 4 * head_cols
    attn_full = [attn_both[:, :wide], attn_both[:, wide:]]
    qkv_pieces = [
        dot_nn(half, attn_full[n]).astype(BF16) for n in streams for half in shifted_one[n]
    ]
    *context_pieces, lse = attend(rows, heads, count, valid, qkv_pieces)
    contexts = (context_pieces[:2], context_pieces[2:])
    ff_full.append(full_weight(unpack(place, after(blocks, context_pieces))))
    attn_sums, middles, shifted_two, middle_rows = ([], [], [], [])
    for n in streams:
        partial = [dot_nt(half, attn_full[n]) for half in contexts[n]]
        attn_sum = add_rows(send_rows(partial[0], partial[1], count))
        middle = inputs[n] + mods[n, 2] * attn_sum
        normed, _ = layer_norm(middle)
        shifted = (normed * (1.0 + mods[n, 4]) + mods[n, 3]).astype(BF16)
        attn_sums.append(attn_sum)
        middles.append(middle)
        middle_rows.append(shifted)
        shifted_two.append(gather_rows(shifted, count))

    def outer_sum(gradient):
        return lax.psum_scatter(gradient, "outer", scatter_dimension=0, tiled=True)

    def owned(summed):
        return exchange(
            [
                lax.dynamic_slice(summed, ((me ^ j) * slab, 0), (slab, summed.shape[1]))
                for j in range(count)
            ],
            count,
        )

    down_ins = finish_both(after(gated, middle_rows[0]), rows[0])
    ff_full[0] = after(ff_full[0], middle_rows[0])
    grad_contexts, grad_middles, partial_rows, proj_ins = ([], [], [], [])
    ff_sums = []
    for n in streams:
        full = ff_full[n] if n == 0 else after(ff_full[n], proj_in, down_partials)
        up_full, down_full = (full[:, :unit_cols], full[:, unit_cols:])
        pairs = [gelu_pair(dot_nn(half, up_full)) for half in shifted_two[n]]
        hidden = [pair[0].astype(BF16) for pair in pairs]

        def down_gradient(where):
            total = dot_tn(where[0], hidden[0]) + dot_tn(where[1], hidden[1])
            return total.astype(BF16)

        grad_ins = down_ins[n]
        if n == 1:
            grad_down = down_gradient(grad_ins)
            grad_ins = after(grad_ins, grad_down)
        grad_pres = [
            (dot_nn(down_in, down_full) * pair[1]).astype(BF16)
            for down_in, pair in zip(grad_ins, pairs)
        ]
        partial = [dot_nt(grad_pre, up_full) for grad_pre in grad_pres]
        sent = send_rows(partial[0], partial[1], count)
        if n == 0:
            grad_down = down_gradient(after(grad_ins, partial))
            partial = (partial, grad_down)
        grad_pres = after(grad_pres, partial)
        total = dot_tn(shifted_two[n][0], grad_pres[0]) + dot_tn(shifted_two[n][1], grad_pres[1])
        grad_up = total.astype(BF16)
        ff_sums.append(outer_sum(jnp.concatenate([grad_down, grad_up], axis=1)))
        grad_middle, proj_in, sums = middle_back(
            place, n, after(sent, grad_up), middles[n], attn_sums[n], cotangents[n], mods
        )
        halves = gather_rows(proj_in, count)
        grad_contexts += [dot_nn(half, attn_full[n]).astype(BF16) for half in halves]
        proj_ins.append(halves)
        grad_middles.append(grad_middle)
        partial_rows.append(sums)
        if n == 0:
            down_partials = [dot_nt(half, down_full) for half in after(hidden, proj_in)]
    down_sent = send_rows(down_partials[0], down_partials[1], count)
    ff_sums[0] = after(ff_sums[0], grad_contexts)

    grad_pieces = attend_back(
        rows, heads, count, valid, qkv_pieces, context_pieces, grad_contexts, lse
    )
    grad_qkv_rows = (grad_pieces[:2], grad_pieces[2:])
    grad_attn = []
    for n in streams:
        grad_attn.append(
            attn_gradient(
                place, 3 * head_cols, shifted_one[n], grad_qkv_rows[n], proj_ins[n], contexts[n]
            )
        )
    attn_grad_sums = [outer_sum(grad_attn[n]) for n in streams]
    grad_qkv_rows = after(grad_qkv_rows, grad_attn)
    partials = [[dot_nt(half, attn_full[n]) for half in grad_qkv_rows[n]] for n in streams]
    sent_one = send_both(partials, count)
    hidden, down_sent = after((hidden, down_sent), partials)
    down_partials = [dot_nt(half, down_full) for half in hidden]
    down_sent = [down_sent, send_rows(down_partials[0], down_partials[1], count)]

    def adam_both(n, before):
        blocks = owned(ff_sums[n])
        return [
            adam_ff(place, blocks, half, *arrays, n, outs)
            for half, arrays, outs in zip((0, 1), (down_all, up_all), before)
        ]

    ff_outs = adam_both(0, ((), ()))
    grad_rows, out_rows, to_owners = end_rows(
        place,
        mods,
        after(sent_one, down_partials, ff_outs[0][0], ff_outs[1][0]),
        [
            (tokens[n], grad_middles[n], cotangents[n], middles[n], partial_rows[n])
            for n in streams
        ],
        down_sent,
        devices,
    )

    received = lax.all_to_all(to_owners, every, split_axis=0, concat_axis=0, tiled=True)
    own_columns = received.reshape(seq_count, cores, 2, column_count).sum(axis=1)
    grad_mod = jnp.einsum(
        "sd,snc->ndc", all_cond.astype(F32), own_columns, precision=lax.Precision.HIGHEST
    )
    grad_bias = jnp.sum(own_columns, axis=0)
    new_mod, mean_mod_next, second_mod_next = adam_step(mod_weight, grad_mod, mean_mod, second_mod)
    new_bias, mean_bias_next, second_bias_next = adam_step(
        mod_bias, grad_bias, mean_bias, second_bias
    )

    core_place = core.astype(jnp.int32)[None]
    image_out, text_out = whole_rows(core_place, out_rows, lengths)
    image_grad, text_grad = whole_rows(core_place, grad_rows, lengths)

    ff_sums[1] = after(ff_sums[1], to_owners)
    ff_outs = adam_both(1, ff_outs)
    down_outs, up_outs = ff_outs
    attn_outs = adam_attn(
        place, owned(after(attn_grad_sums[0], to_owners)), qkv_all, proj_all, 0, ()
    )
    last_sum = after(
        attn_grad_sums[1], attn_outs[0], up_outs[0], down_outs[0], new_mod, text_out, text_grad
    )
    attn_outs = adam_attn(place, owned(last_sum), qkv_all, proj_all, 1, attn_outs)
    grad_up, new_up, mean_up_next, second_up_next = up_outs
    grad_down, new_down, mean_down_next, second_down_next = (
        a.transpose(0, 2, 1) for a in down_outs
    )
    grad_qkv, new_qkv, mean_qkv_next, second_qkv_next = (
        a.transpose(0, 2, 1, 3) for a in attn_outs[:4]
    )
    grad_proj, new_proj, mean_proj_next, second_proj_next = (
        a.transpose(0, 2, 1) for a in attn_outs[4:]
    )
    return (
        image_out,
        text_out,
        image_grad,
        text_grad,
        grad_mod,
        grad_bias,
        grad_qkv,
        grad_proj,
        grad_up,
        grad_down,
        new_mod,
        new_bias,
        new_qkv,
        new_proj,
        new_up,
        new_down,
        mean_mod_next,
        second_mod_next,
        mean_bias_next,
        second_bias_next,
        mean_qkv_next,
        second_qkv_next,
        mean_proj_next,
        second_proj_next,
        mean_up_next,
        second_up_next,
        mean_down_next,
        second_down_next,
    )


def solution(mesh):
    dp, cores = mesh.devices.shape
    inner = math.gcd(dp, INNER)
    split = Mesh(mesh.devices.reshape(dp // inner, inner, cores), ("outer", "inner", "tensor"))
    group = ("outer", "inner")
    every = ("outer", "inner", "tensor")
    tokens = P(group, None, None)
    mod, bias = (P(None, None, every), P(None, every))
    qkv = P(None, group, None, "tensor")
    columns = P(None, group, "tensor")
    rows = P(None, "tensor", group)
    return jax.shard_map(
        local,
        mesh=split,
        in_specs=(tokens,) * 4
        + (P(),)
        + (mod, bias, qkv, rows, columns, rows)
        + (mod, mod, bias, bias, qkv, qkv, rows, rows, columns, columns, rows, rows),
        out_specs=(tokens,) * 4
        + (mod, bias, qkv, rows, columns, rows)
        + (mod, bias, qkv, rows, columns, rows)
        + (mod, mod, bias, bias, qkv, qkv, rows, rows, columns, columns, rows, rows),
        check_vma=False,
    )
```

profile of v0, /device:TPU:0, one launch (start us, length us, event | category | flops | bytes accessed | tf_op | source)
XLA Modules:
  0.0 656.2 jit_solution(17921603976800040976)
XLA Ops:
  14.7 6.5 collective-permute-done.refs_1_
  21.3 6.9 %collective-permute-done.1.refs_2_ = bf16[96,1536]{1,0:T(8,128)(2,1)S(1)} collective-permute-done((bf16[96,1536]{1,0:T(8,128)(2,1)}, bf16[96,1536]{1,0:T(8,128)(2,1)S(1)}, u32[]{:S(2)}, u32[]{:S(2)}) %collective-permute-start.1) | collective-permute-done | bytes 294944 | tf_op jit(solution)/shard_map/ppermute | solution.py:234
  41.6 10.6 %all-to-all-done = f32[32,2,288]{2,1,0:T(2,128)S(1)} async-done(((f32[32,2,288]{2,1,0:T(2,128)}), f32[32,2,288]{2,1,0:T(2,128)S(1)}, u32[]{:S(2)}, u32[]{:S(2)}) %all-to-all-start) | async-done | bytes 73760 | tf_op jit(solution)/shard_map/all_to_all | solution.py:730
  56.6 14.7 %collective-permute-done.5 = bf16[208,1536]{1,0:T(8,128)(2,1)S(1)} collective-permute-done((bf16[208,1536]{1,0:T(8,128)(2,1)S(1)}, bf16[208,1536]{1,0:T(8,128)(2,1)S(1)}, u32[]{:S(2)}, u32[]{:S(2)}) %collective-permute-start.5) | collective-permute-done | bytes 639008 | tf_op jit(solution)/shard_map/ppermute | solution.py:234
  71.4 11.8 %collective-permute-done.4 = bf16[208,1536]{1,0:T(8,128)(2,1)S(1)} collective-permute-done((bf16[208,1536]{1,0:T(8,128)(2,1)S(1)}, bf16[208,1536]{1,0:T(8,128)(2,1)S(1)}, u32[]{:S(2)}, u32[]{:S(2)}) %collective-permute-start.4) | collective-permute-done | bytes 639008 | tf_op jit(solution)/shard_map/ppermute | solution.py:234
  95.2 28.0 %all-gather.4.cloned.1.call-done = bf16[1536,1536]{1,0:T(8,128)(2,1)} async-done(((bf16[384,1536]{1,0:T(8,128)(2,1)}), bf16[1536,1536]{1,0:T(8,128)(2,1)}) %all-gather.4.cloned.1.call-update) | async-done | bytes 4718608 | tf_op jit(solution)/shard_map/all_gather | solution.py:712
  135.9 20.6 %attend.1 = (bf16[512,768]{1,0:T(8,128)(2,1)}, bf16[512,768]{1,0:T(8,128)(2,1)}, bf16[320,768]{1,0:T(8,128)(2,1)}, bf16[320,768]{1,0:T(8,128)(2,1)}, f32[4,416,128]{2,1,0:T(8,128)}) custom-call(s32[2]{0:T(128)} %pad_add_fusion.valid_ref, bf16[512,768]{1,0:T(8,128)(2,1)} %convolution_convert_fusion.5.refs_0_, ...), custom_call_target="tpu_custom_call" | custom-call | flops 531628032 | bytes 2555904 | tf_op jit(solution)/shard_map/attend/pallas_call | solution.py:177
  174.4 6.5 collective-permute-done.12
  180.9 8.4 %collective-permute-done.14 = bf16[128,1536]{1,0:T(8,128)(2,1)S(1)} collective-permute-done((bf16[128,1536]{1,0:T(8,128)(2,1)S(1)}, bf16[128,1536]{1,0:T(8,128)(2,1)S(1)}, u32[]{:S(2)}, u32[]{:S(2)}) %collective-permute-start.14) | collective-permute-done | bytes 393248 | tf_op jit(solution)/shard_map/ppermute | solution.py:234
  200.4 5.1 collective-permute-done.20
  206.0 7.9 %collective-permute-done.19 = bf16[128,1536]{1,0:T(8,128)(2,1)} collective-permute-done((bf16[128,1536]{1,0:T(8,128)(2,1)S(1)}, bf16[128,1536]{1,0:T(8,128)(2,1)}, u32[]{:S(2)}, u32[]{:S(2)}) %collective-permute-start.19) | collective-permute-done | bytes 393248 | tf_op jit(solution)/shard_map/ppermute | solution.py:234
  228.1 10.0 %collective-permute-done.16 = bf16[208,1536]{1,0:T(8,128)(2,1)S(1)} collective-permute-done((bf16[208,1536]{1,0:T(8,128)(2,1)S(1)}, bf16[208,1536]{1,0:T(8,128)(2,1)S(1)}, u32[]{:S(2)}, u32[]{:S(2)}) %collective-permute-start.16) | collective-permute-done | bytes 639008 | tf_op jit(solution)/shard_map/ppermute | solution.py:234
  299.0 8.0 %collective-permute-done.25.refs_1_ = bf16[128,1536]{1,0:T(8,128)(2,1)} collective-permute-done((bf16[128,1536]{1,0:T(8,128)(2,1)S(1)}, bf16[128,1536]{1,0:T(8,128)(2,1)}, u32[]{:S(2)}, u32[]{:S(2)}) %collective-permute-start.25) | collective-permute-done | bytes 393248 | tf_op jit(solution)/shard_map/ppermute | solution.py:234
  307.8 5.7 shard_map.442
  345.5 5.7 fusion.126
  401.6 6.6 %collective-permute-done.48 = bf16[80,1536]{1,0:T(8,128)(2,1)S(1)} collective-permute-done((bf16[80,1536]{1,0:T(8,128)(2,1)}, bf16[80,1536]{1,0:T(8,128)(2,1)S(1)}, u32[]{:S(2)}, u32[]{:S(2)}) %collective-permute-start.48) | collective-permute-done | bytes 245792 | tf_op jit(solution)/shard_map/ppermute | solution.py:234
  420.4 19.2 %attend_back.1 = (bf16[512,768]{1,0:T(8,128)(2,1)}, bf16[512,768]{1,0:T(8,128)(2,1)}, bf16[320,768]{1,0:T(8,128)(2,1)}, bf16[320,768]{1,0:T(8,128)(2,1)}) custom-call(s32[2]{0:T(128)} %pad_add_fusion.valid_ref, bf16[512,768]{1,0:T(8,128)(2,1)} %convolution_convert_fusion.5.refs_0_, bf16[512,768]{1,0:T(8,128)(2,1)} %convolution_convert_fusion.4.refs_1_, ...), custom_call_target="tpu_custom_call" | custom-call | flops 1329070080 | bytes 6389760 | tf_op jit(solution)/shard_map/attend_back/pallas_call | solution.py:203
  439.5 8.1 %shard_map.446 = bf16[1536,768]{1,0:T(8,128)(2,1)} custom-call(s32[1]{0:T(128)} %bitcast.1.me_ref, bf16[512,1536]{1,0:T(8,128)(2,1)} %copy-done.7, bf16[512,1536]{1,0:T(8,128)(2,1)} %collective-permute-done.6.refs_1_, bf16[512,768]{1,0:T(8,128)(2,1)} %get-tuple-element.202.refs_2_, bf16[512,768]{1,0:T(8,128)(2,1)} %get-tuple-element.203.refs_3_, ...), custom_call_target="tpu_custom_call" | custom-call | flops 2415919104 | bytes 6291456 | tf_op jit(solution)/shard_map/pallas_call | solution.py:648
  452.1 7.1 %shard_map.447 = bf16[1536,768]{1,0:T(8,128)(2,1)} custom-call(s32[1]{0:T(128)} %bitcast.1.me_ref, bf16[320,1536]{1,0:T(8,128)(2,1)} %pad_maximum_fusion.6.refs_0_, bf16[320,1536]{1,0:T(8,128)(2,1)} %collective-permute-done.7.refs_1_, bf16[320,768]{1,0:T(8,128)(2,1)} %get-tuple-element.205.refs_2_, bf16[320,768]{1,0:T(8,128)(2,1)} %get-tuple-element.204.refs_3_, ...), custom_call_target="tpu_custom_call" | custom-call | flops 1509949440 | bytes 3932160 | tf_op jit(solution)/shard_map/pallas_call | solution.py:648
  474.9 5.3 fusion.127
  493.7 23.6 %collective-permute-done.57.refs_3_ = bf16[208,1536]{1,0:T(8,128)(2,1)} collective-permute-done((bf16[208,1536]{1,0:T(8,128)(2,1)S(1)}, bf16[208,1536]{1,0:T(8,128)(2,1)}, u32[]{:S(2)}, u32[]{:S(2)}) %collective-permute-start.57) | collective-permute-done | bytes 639008 | tf_op jit(solution)/shard_map/ppermute | solution.py:234
  525.3 12.9 %collective-permute-done.54.refs_2_ = bf16[96,1536]{1,0:T(8,128)(2,1)S(1)} collective-permute-done((bf16[96,1536]{1,0:T(8,128)(2,1)S(1)}, bf16[96,1536]{1,0:T(8,128)(2,1)S(1)}, u32[]{:S(2)}, u32[]{:S(2)}) %collective-permute-start.54) | collective-permute-done | bytes 294944 | tf_op jit(solution)/shard_map/ppermute | solution.py:234
  547.0 5.1 shard_map.449
  552.1 5.1 shard_map.448
  557.3 9.3 %shard_map.450 = (f32[208,1536]{1,0:T(8,128)}, f32[208,1536]{1,0:T(8,128)}, f32[32,2,288]{2,1,0:T(2,128)}) custom-call(s32[1]{0:T(128)} %bitcast.1.me_ref, f32[2,6,1536]{2,1,0:T(8,128)} %copy-done.23, bf16[208,1536]{1,0:T(8,128)(2,1)} %collective-permute-done.52.refs_1_, bf16[208,1536]{1,0:T(8,128)(2,1)} %collective-permute-done.56.refs_2_, ...), custom_call_target="tpu_custom_call" | custom-call | tf_op jit(solution)/shard_map/pallas_call | solution.py:477
  575.5 6.0 all-to-all-done.1
  588.0 10.1 %multiply_subtract_fusion = (f32[2,1536,288]{1,2,0:T(8,128)}, f32[2,1536,288]{1,2,0:T(8,128)}, f32[2,1536,288]{1,2,0:T(8,128)}, f32[2,1536,288]{1,2,0:T(8,128)}) fusion(f32[2,1536,288]{1,2,0:T(8,128)} %param.28, f32[2,1536,288]{1,2,0:T(8,128)} %param.34, f32[2,1536,288]{1,2,0:T(8,128)} %param.35, f32[16,768]{1,0:T(8,128)S(1)} %copy-done.87, ...), kind=kOutput, calls=%fused_computation.8 | convolution fusion | flops 183287808 | bytes 24907776 | tf_op jit(solution)/shard_map/sd,snc->ndc/dot_general | solution.py:882
  598.1 5.2 shard_map.453
  613.0 5.1 shard_map.455
  618.1 5.2 shard_map.454
  623.3 8.6 %reduce-scatter.7.cloned.1.call-done = bf16[384,768]{1,0:T(8,128)(2,1)} async-done(((bf16[1536,768]{1,0:T(8,128)(2,1)}), bf16[384,768]{1,0:T(8,128)(2,1)}) %reduce-scatter.7.cloned.1.call-update) | async-done | bytes 589840 | tf_op jit(solution)/shard_map/reduce_scatter | solution.py:786
  643.7 5.2 shard_map.456
  (543 shorter events, 335.9 us)
Async XLA Ops:
  7.2 115.9 %all-gather.4.cloned.1.call-start = ((), (), s32[]{:S(2)}) async-start(), calls=%async_computation.6 | async-start | bytes 5898240 | tf_op jit(solution)/shard_map/all_gather | solution.py:712
  40.7 225.2 %all-gather.6.cloned.1.call-start = ((), (), s32[]{:S(2)}) async-start(), calls=%async_computation.7 | async-start | bytes 5898240 | tf_op jit(solution)/shard_map/all_gather | solution.py:712
  54.2 29.0 %collective-permute-start.4 = (bf16[208,1536]{1,0:T(8,128)(2,1)S(1)}, bf16[208,1536]{1,0:T(8,128)(2,1)S(1)}, u32[]{:S(2)}, u32[]{:S(2)}) collective-permute-start(bf16[208,1536]{1,0:T(8,128)(2,1)S(1)} %pad_maximum_fusion.9), channel_id=1, source_target_pairs={{0,4},{2,6},{4,0},{6,2},{1,5},{3,7},{5,1},{7,3},{8,12},{10,14},{12... | collective-permute-start | bytes 1916936 | tf_op jit(solution)/shard_map/ppermute | solution.py:234
  54.7 28.5 %collective-permute-start.3 = (bf16[208,1536]{1,0:T(8,128)(2,1)S(1)}, bf16[208,1536]{1,0:T(8,128)(2,1)S(1)}, u32[]{:S(2)}, u32[]{:S(2)}) collective-permute-start(bf16[208,1536]{1,0:T(8,128)(2,1)S(1)} %pad_maximum_fusion.9), channel_id=1, source_target_pairs={{0,2},{2,0},{4,6},{6,4},{1,3},{3,1},{5,7},{7,5},{8,10},{10,8},{12,... | collective-permute-start | bytes 1916936 | tf_op jit(solution)/shard_map/ppermute | solution.py:234
  91.7 69.3 %collective-permute-start.8 = (bf16[96,1536]{1,0:T(8,128)(2,1)}, bf16[96,1536]{1,0:T(8,128)(2,1)S(1)}, u32[]{:S(2)}, u32[]{:S(2)}) collective-permute-start(bf16[96,1536]{1,0:T(8,128)(2,1)} %get-tuple-element.157), channel_id=1, source_target_pairs={{0,2},{2,0},{4,6},{6,4},{1,3},{3,1},{5,7},{7,5},{8,10},{10,8},{12,... | collective-permute-start | bytes 884744 | tf_op jit(solution)/shard_map/ppermute | solution.py:234
  93.3 67.8 %collective-permute-start.9 = (bf16[96,1536]{1,0:T(8,128)(2,1)}, bf16[96,1536]{1,0:T(8,128)(2,1)}, u32[]{:S(2)}, u32[]{:S(2)}) collective-permute-start(bf16[96,1536]{1,0:T(8,128)(2,1)} %get-tuple-element.158), channel_id=1, source_target_pairs={{0,4},{2,6},{4,0},{6,2},{1,5},{3,7},{5,1},{7,3},{8,12},{10,14},{12... | collective-permute-start | bytes 884744 | tf_op jit(solution)/shard_map/ppermute | solution.py:234
  93.8 67.2 %collective-permute-start.10 = (bf16[96,1536]{1,0:T(8,128)(2,1)}, bf16[96,1536]{1,0:T(8,128)(2,1)}, u32[]{:S(2)}, u32[]{:S(2)}) collective-permute-start(bf16[96,1536]{1,0:T(8,128)(2,1)} %get-tuple-element.159), channel_id=1, source_target_pairs={{0,6},{2,4},{4,2},{6,0},{1,7},{3,5},{5,3},{7,1},{8,14},{10,12},{12... | collective-permute-start | bytes 884744 | tf_op jit(solution)/shard_map/ppermute | solution.py:234
  164.2 187.1 %all-gather.8.cloned.1.call-start = ((), (), s32[]{:S(2)}) async-start(), calls=%async_computation.8 | async-start | bytes 5898240 | tf_op jit(solution)/shard_map/all_gather | solution.py:712
  174.4 44.0 %collective-permute-start.31 = (bf16[320,1536]{1,0:T(8,128)(2,1)}, bf16[320,1536]{1,0:T(8,128)(2,1)}, u32[]{:S(2)}, u32[]{:S(2)}) collective-permute-start(bf16[320,1536]{1,0:T(8,128)(2,1)} %convolution_convert_fusion.1), channel_id=1, source_target_pairs={{0,1},{1,0},{2,3},{3,2},{4,5},{5,4},{6,7},{7,6},{8,9},{9,8},{10,11... | collective-permute-start | bytes 2949128 | tf_op jit(solution)/shard_map/ppermute | solution.py:230
  196.0 31.4 %collective-permute-start.17 = (bf16[208,1536]{1,0:T(8,128)(2,1)S(1)}, bf16[208,1536]{1,0:T(8,128)(2,1)S(1)}, u32[]{:S(2)}, u32[]{:S(2)}) collective-permute-start(bf16[208,1536]{1,0:T(8,128)(2,1)S(1)} %pad_maximum_fusion.10), channel_id=1, source_target_pairs={{0,6},{2,4},{4,2},{6,0},{1,7},{3,5},{5,3},{7,1},{8,14},{10,12},{12... | collective-permute-start | bytes 1916936 | tf_op jit(solution)/shard_map/ppermute | solution.py:234
  205.4 32.6 %collective-permute-start.16 = (bf16[208,1536]{1,0:T(8,128)(2,1)S(1)}, bf16[208,1536]{1,0:T(8,128)(2,1)S(1)}, u32[]{:S(2)}, u32[]{:S(2)}) collective-permute-start(bf16[208,1536]{1,0:T(8,128)(2,1)S(1)} %pad_maximum_fusion.10), channel_id=1, source_target_pairs={{0,4},{2,6},{4,0},{6,2},{1,5},{3,7},{5,1},{7,3},{8,12},{10,14},{12... | collective-permute-start | bytes 1916936 | tf_op jit(solution)/shard_map/ppermute | solution.py:234
  213.9 26.4 %collective-permute-start.15 = (bf16[208,1536]{1,0:T(8,128)(2,1)S(1)}, bf16[208,1536]{1,0:T(8,128)(2,1)S(1)}, u32[]{:S(2)}, u32[]{:S(2)}) collective-permute-start(bf16[208,1536]{1,0:T(8,128)(2,1)S(1)} %pad_maximum_fusion.10), channel_id=1, source_target_pairs={{0,2},{2,0},{4,6},{6,4},{1,3},{3,1},{5,7},{7,5},{8,10},{10,8},{12,... | collective-permute-start | bytes 1916936 | tf_op jit(solution)/shard_map/ppermute | solution.py:234
  215.4 30.9 %collective-permute-start.38 = (bf16[96,1536]{1,0:T(8,128)(2,1)}, bf16[96,1536]{1,0:T(8,128)(2,1)S(1)}, u32[]{:S(2)}, u32[]{:S(2)}) collective-permute-start(bf16[96,1536]{1,0:T(8,128)(2,1)} %get-tuple-element.179), channel_id=1, source_target_pairs={{0,2},{2,0},{4,6},{6,4},{1,3},{3,1},{5,7},{7,5},{8,10},{10,8},{12,... | collective-permute-start | bytes 884744 | tf_op jit(solution)/shard_map/ppermute | solution.py:234
  218.4 47.5 %collective-permute-start.22 = (bf16[512,1536]{1,0:T(8,128)(2,1)}, bf16[512,1536]{1,0:T(8,128)(2,1)}, u32[]{:S(2)}, u32[]{:S(2)}) collective-permute-start(bf16[512,1536]{1,0:T(8,128)(2,1)} %pad_maximum_fusion.5), channel_id=1, source_target_pairs={{0,1},{1,0},{2,3},{3,2},{4,5},{5,4},{6,7},{7,6},{8,9},{9,8},{10,11... | collective-permute-start | bytes 4718600 | tf_op jit(solution)/shard_map/ppermute | solution.py:230
  241.9 28.0 %collective-permute-start.21 = (bf16[512,1536]{1,0:T(8,128)(2,1)S(1)}, bf16[512,1536]{1,0:T(8,128)(2,1)}, u32[]{:S(2)}, u32[]{:S(2)}) collective-permute-start(bf16[512,1536]{1,0:T(8,128)(2,1)S(1)} %pad_maximum_fusion.4), channel_id=1, source_target_pairs={{0,1},{1,0},{2,3},{3,2},{4,5},{5,4},{6,7},{7,6},{8,9},{9,8},{10,11... | collective-permute-start | bytes 4718600 | tf_op jit(solution)/shard_map/ppermute | solution.py:230
  256.6 231.6 %reduce-scatter.5.cloned.1.call-start = ((), (), s32[]{:S(2)}) async-start(), calls=%async_computation.9 | async-start | bytes 5898240 | tf_op jit(solution)/shard_map/reduce_scatter | solution.py:786
  318.1 26.4 %collective-permute-start.58 = (bf16[512,1536]{1,0:T(8,128)(2,1)}, bf16[512,1536]{1,0:T(8,128)(2,1)}, u32[]{:S(2)}, u32[]{:S(2)}) collective-permute-start(bf16[512,1536]{1,0:T(8,128)(2,1)} %fusion.41), channel_id=1, source_target_pairs={{0,1},{1,0},{2,3},{3,2},{4,5},{5,4},{6,7},{7,6},{8,9},{9,8},{10,11... | collective-permute-start | bytes 4718600 | tf_op jit(solution)/shard_map/ppermute | solution.py:230
  324.4 245.3 %reduce-scatter.9.cloned.1.call-start = ((), (), s32[]{:S(2)}) async-start(), calls=%async_computation.11 | async-start | bytes 2949120 | tf_op jit(solution)/shard_map/reduce_scatter | solution.py:786
  340.1 28.3 %collective-permute-start.29 = (bf16[128,1536]{1,0:T(8,128)(2,1)}, bf16[128,1536]{1,0:T(8,128)(2,1)}, u32[]{:S(2)}, u32[]{:S(2)}) collective-permute-start(bf16[128,1536]{1,0:T(8,128)(2,1)} %get-tuple-element.175), channel_id=1, source_target_pairs={{0,6},{2,4},{4,2},{6,0},{1,7},{3,5},{5,3},{7,1},{8,14},{10,12},{12... | collective-permute-start | bytes 1179656 | tf_op jit(solution)/shard_map/ppermute | solution.py:234
  370.2 43.1 %collective-permute-start.30 = (bf16[512,1536]{1,0:T(8,128)(2,1)}, bf16[512,1536]{1,0:T(8,128)(2,1)}, u32[]{:S(2)}, u32[]{:S(2)}) collective-permute-start(bf16[512,1536]{1,0:T(8,128)(2,1)} %constant_dynamic-update-slice_fusion.refs_4_), channel_id=1, source_target_pairs={{0,1},{1,0},{2,3},{3,2},{4,5},{5,4},{6,7},{7,6},{8,9},{9,8},{10,11... | collective-permute-start | bytes 4718600 | tf_op jit(solution)/shard_map/ppermute | solution.py:230
  447.7 133.9 %reduce-scatter.11.cloned.1.call-start = ((), (), s32[]{:S(2)}) async-start(), calls=%async_computation.12 | async-start | bytes 5898240 | tf_op jit(solution)/shard_map/reduce_scatter | solution.py:786
  451.9 180.0 %reduce-scatter.7.cloned.1.call-start = ((), (), s32[]{:S(2)}) async-start(), calls=%async_computation.10 | async-start | bytes 2949120 | tf_op jit(solution)/shard_map/reduce_scatter | solution.py:786
  482.4 74.9 %collective-permute-start.52 = (bf16[208,1536]{1,0:T(8,128)(2,1)}, bf16[208,1536]{1,0:T(8,128)(2,1)}, u32[]{:S(2)}, u32[]{:S(2)}) collective-permute-start(bf16[208,1536]{1,0:T(8,128)(2,1)} %pad_maximum_fusion.11), channel_id=1, source_target_pairs={{0,2},{2,0},{4,6},{6,4},{1,3},{3,1},{5,7},{7,5},{8,10},{10,8},{12,... | collective-permute-start | bytes 1916936 | tf_op jit(solution)/shard_map/ppermute | solution.py:234
  484.1 33.2 %collective-permute-start.57 = (bf16[208,1536]{1,0:T(8,128)(2,1)S(1)}, bf16[208,1536]{1,0:T(8,128)(2,1)}, u32[]{:S(2)}, u32[]{:S(2)}) collective-permute-start(bf16[208,1536]{1,0:T(8,128)(2,1)S(1)} %pad_maximum_fusion.13), channel_id=1, source_target_pairs={{0,6},{2,4},{4,2},{6,0},{1,7},{3,5},{5,3},{7,1},{8,14},{10,12},{12... | collective-permute-start | bytes 1916936 | tf_op jit(solution)/shard_map/ppermute | solution.py:234
  490.3 66.9 %collective-permute-start.56 = (bf16[208,1536]{1,0:T(8,128)(2,1)}, bf16[208,1536]{1,0:T(8,128)(2,1)}, u32[]{:S(2)}, u32[]{:S(2)}) collective-permute-start(bf16[208,1536]{1,0:T(8,128)(2,1)} %pad_maximum_fusion.12), channel_id=1, source_target_pairs={{0,4},{2,6},{4,0},{6,2},{1,5},{3,7},{5,1},{7,3},{8,12},{10,14},{12... | collective-permute-start | bytes 1916936 | tf_op jit(solution)/shard_map/ppermute | solution.py:234
  491.5 32.0 %collective-permute-start.55 = (bf16[96,1536]{1,0:T(8,128)(2,1)S(1)}, bf16[96,1536]{1,0:T(8,128)(2,1)S(1)}, u32[]{:S(2)}, u32[]{:S(2)}) collective-permute-start(bf16[96,1536]{1,0:T(8,128)(2,1)S(1)} %get-tuple-element.404), channel_id=1, source_target_pairs={{0,6},{2,4},{4,2},{6,0},{1,7},{3,5},{5,3},{7,1},{8,14},{10,12},{12... | collective-permute-start | bytes 884744 | tf_op jit(solution)/shard_map/ppermute | solution.py:234
  493.3 45.0 %collective-permute-start.54 = (bf16[96,1536]{1,0:T(8,128)(2,1)S(1)}, bf16[96,1536]{1,0:T(8,128)(2,1)S(1)}, u32[]{:S(2)}, u32[]{:S(2)}) collective-permute-start(bf16[96,1536]{1,0:T(8,128)(2,1)S(1)} %get-tuple-element.405), channel_id=1, source_target_pairs={{0,4},{2,6},{4,0},{6,2},{1,5},{3,7},{5,1},{7,3},{8,12},{10,14},{12... | collective-permute-start | bytes 884744 | tf_op jit(solution)/shard_map/ppermute | solution.py:234
  523.5 33.8 %collective-permute-start.65 = (bf16[80,1536]{1,0:T(8,128)(2,1)}, bf16[80,1536]{1,0:T(8,128)(2,1)}, u32[]{:S(2)}, u32[]{:S(2)}) collective-permute-start(bf16[80,1536]{1,0:T(8,128)(2,1)} %get-tuple-element.408), channel_id=1, source_target_pairs={{0,6},{2,4},{4,2},{6,0},{1,7},{3,5},{5,3},{7,1},{8,14},{10,12},{12... | collective-permute-start | bytes 737288 | tf_op jit(solution)/shard_map/ppermute | solution.py:234
  575.0 28.3 %collective-permute-start.66 = (f32[208,1536]{1,0:T(8,128)}, f32[208,1536]{1,0:T(8,128)S(1)}, u32[]{:S(2)}, u32[]{:S(2)}) collective-permute-start(f32[208,1536]{1,0:T(8,128)} %get-tuple-element.224.own), channel_id=1, source_target_pairs={{0,1},{1,0},{2,3},{3,2},{4,5},{5,4},{6,7},{7,6},{8,9},{9,8},{10,11... | collective-permute-start | bytes 3833864 | tf_op jit(solution)/shard_map/ppermute | solution.py:230
  575.0 32.7 %collective-permute-start.67 = (f32[208,1536]{1,0:T(8,128)}, f32[208,1536]{1,0:T(8,128)S(1)}, u32[]{:S(2)}, u32[]{:S(2)}) collective-permute-start(f32[208,1536]{1,0:T(8,128)} %get-tuple-element.227.own), channel_id=1, source_target_pairs={{0,1},{1,0},{2,3},{3,2},{4,5},{5,4},{6,7},{7,6},{8,9},{9,8},{10,11... | collective-permute-start | bytes 3833864 | tf_op jit(solution)/shard_map/ppermute | solution.py:230
  584.5 27.7 %collective-permute-start.73 = (bf16[96,1536]{1,0:T(8,128)(2,1)}, bf16[96,1536]{1,0:T(8,128)(2,1)S(1)}, u32[]{:S(2)}, u32[]{:S(2)}) collective-permute-start(bf16[96,1536]{1,0:T(8,128)(2,1)} %get-tuple-element.400), channel_id=1, source_target_pairs={{0,6},{2,4},{4,2},{6,0},{1,7},{3,5},{5,3},{7,1},{8,14},{10,12},{12... | collective-permute-start | bytes 884744 | tf_op jit(solution)/shard_map/ppermute | solution.py:234
  586.6 25.6 %collective-permute-start.72 = (bf16[96,1536]{1,0:T(8,128)(2,1)}, bf16[96,1536]{1,0:T(8,128)(2,1)S(1)}, u32[]{:S(2)}, u32[]{:S(2)}) collective-permute-start(bf16[96,1536]{1,0:T(8,128)(2,1)} %get-tuple-element.401), channel_id=1, source_target_pairs={{0,4},{2,6},{4,0},{6,2},{1,5},{3,7},{5,1},{7,3},{8,12},{10,14},{12... | collective-permute-start | bytes 884744 | tf_op jit(solution)/shard_map/ppermute | solution.py:234
  (172 other events, 2362.6 us)
Sparse Core Ops, SparseCore 0:
  31.5 91.5 all-gather.3
  164.3 87.9 all-gather.5
  256.7 87.9 all-gather.7
  346.9 83.6 reduce-scatter.4
  447.8 45.1 reduce-scatter.8
  495.1 86.1 reduce-scatter.10
  583.6 48.2 reduce-scatter.6
where the time goes:
time: 663 us; the launch traced here: 656 us
  waiting for transfers between devices  231 us (35%)
  Pallas kernels  128 us (19%)
  matrix products  126 us (19%)
  starting transfers between devices  81.1 us (12%)
  local copies, waits for them, and re-layouts  51.1 us (8%)
  other arithmetic  22.8 us (3%)
  between operations  16.3 us (2%)
    ppermute x60, waiting for transfers between devices, hop(): lax.ppermute(values, 'inner', [(i, i ^ distance) for i in range(count)])  175 us
    ppermute x60, starting transfers between devices, hop(): lax.ppermute(values, 'inner', [(i, i ^ distance) for i in range(count)])  70.2 us
    dot_general x16, matrix products, dot_nt(): lax.dot_general(a, b, (((1,), (1,)), ((), ())), preferred_element_type=F32)  47.3 us
    dot_general x16, matrix products, dot_nn(): lax.dot_general(a, b, (((1,), (0,)), ((), ())), preferred_element_type=F32)  45.3 us
    all_gather x3, waiting for transfers between devices, full_weight(): return lax.all_gather(shard, 'outer', axis=0, tiled=True)  28 us
    pallas_call x5, Pallas kernels, row_kernel(): pl.pallas_call(body, grid_spec=pltpu.PrefetchScalarGridSpec(num_scalar_pr...  25.9 us
    unnamed x244, local copies, waits for them, and re-layouts  24.4 us
    pallas_call x1, Pallas kernels, attend(): pl.pallas_call(functools.partial(attend_kernel, rows, heads, padded), gri...  20.6 us
  transfers between devices with their start and end apart: 86, of which 36 were waited for; matrix products, arithmetic and copies ran while one was open for 28% of the time, Pallas kernels for 18%

commit v1 on v0

--- a/solution.py
+++ b/solution.py
@@ -379,6 +379,38 @@
     )(me, *blocks)
 
 
+def merge_kernel(count, me_ref, own_ref, others_ref, out):
+    slab = own_ref.shape[0]
+
+    def place(number):
+        for j in range(count):
+            at = (j ^ number) * slab
+            if j == 0:
+                out[at : at + slab, :] = own_ref[...]
+            else:
+                out[at : at + slab, :] = others_ref[(j - 1) * slab : j * slab, :]
+
+    by_place(me_ref, count, place)
+
+
+def merge(me, own, others, slab, count):
+    columns = own.shape[1]
+    outer = own.shape[0] // slab
+    return pl.pallas_call(
+        functools.partial(merge_kernel, count),
+        grid_spec=pltpu.PrefetchScalarGridSpec(
+            num_scalar_prefetch=1,
+            grid=(outer,),
+            in_specs=[
+                pl.BlockSpec((slab, columns), lambda i, m: (i, 0)),
+                pl.BlockSpec(((count - 1) * slab, columns), lambda i, m: (i, 0)),
+            ],
+            out_specs=pl.BlockSpec((count * slab, columns), lambda i, m: (i, 0)),
+        ),
+        out_shape=jax.ShapeDtypeStruct((outer * count * slab, columns), BF16),
+    )(me, own, others)
+
+
 def adam_refs(gradient, weight, mean, second, outs):
     updated, mean_new, second_new = adam_step(weight, gradient, mean, second)
     for out, value in zip(outs, (gradient, updated, mean_new, second_new)):
@@ -418,47 +450,48 @@
     )(me, *blocks, weight, mean, second, *before)
 
 
-def adam_attn_kernel(count, me_ref, *refs):
-    blocks, weights = (refs[:count], refs[count : count + 6])
-    qkv_outs, proj_outs = (refs[-10:-6], refs[-6:-2])
-    qkv_grad, proj_grad = refs[-2:]
-    columns = proj_grad.shape[1] // count
+def adam_attn_kernel(count, parts, me_ref, *refs):
+    blocks, (weight, mean, second) = (refs[:count], refs[count : count + 3])
+    outs, gradient = (refs[-5:-1], refs[-1])
+    columns = gradient.shape[1] // count
+    step = pl.program_id(0)
 
     def place(number):
-        for j, block in enumerate(blocks):
-            at = (j ^ number) * columns
-            for k in range(3):
-                qkv_grad[k, :, at : at + columns] = block[
-                    :, k * columns : (k + 1) * columns
-                ].astype(F32)
-            proj_grad[:, at : at + columns] = block[:, 3 * columns :].astype(F32)
+        for k in range(parts):
+
+            @pl.when(step == k)
+            def take(k=k):
+                for j, block in enumerate(blocks):
+                    at = (j ^ number) * columns
+                    gradient[:, at : at + columns] = block[
+                        :, k * columns : (k + 1) * columns
+                    ].astype(F32)
 
     by_place(me_ref, count, place)
-    adam_refs(qkv_grad[...], weights[0][...], weights[1][...], weights[2][...], qkv_outs)
-    adam_refs(proj_grad[...], weights[3][...], weights[4][...], weights[5][...], proj_outs)
-
-
-def adam_attn(me, blocks, qkv, proj, n, before):
-    count = len(blocks)
-    slab, full = proj[0].shape[1:]
-    qkv_spec = pl.BlockSpec((None, 3, slab, full), lambda i, m: (n, 0, 0, 0))
-    proj_spec = pl.BlockSpec((None, slab, full), lambda i, m: (n, 0, 0))
+    adam_refs(gradient[...], weight[...], mean[...], second[...], outs)
+
+
+def adam_attn(me, count, blocks, weight, mean, second):
+    parts, slab, full = weight.shape
+    size = blocks[0].shape[1] * len(blocks) // count
+    places = [j if len(blocks) == 1 else 0 for j in range(count)]
+    blocks = blocks * (count // len(blocks))
+    spec = pl.BlockSpec((None, slab, full), lambda k, m: (k, 0, 0))
     return pl.pallas_call(
-        functools.partial(adam_attn_kernel, count),
+        functools.partial(adam_attn_kernel, count, parts),
         grid_spec=pltpu.PrefetchScalarGridSpec(
             num_scalar_prefetch=1,
-            grid=(1,),
-            in_specs=[pl.BlockSpec(blocks[0].shape, lambda i, m: (0, 0))] * count
-            + [qkv_spec] * 3
-            + [proj_spec] * 3
-            + [pl.BlockSpec(memory_space=pl.ANY)] * len(before),
-            out_specs=[qkv_spec] * 4 + [proj_spec] * 4,
-            scratch_shapes=[pltpu.VMEM((3, slab, full), F32), pltpu.VMEM((slab, full), F32)],
-        ),
-        out_shape=[jax.ShapeDtypeStruct(qkv[0].shape, F32)] * 4
-        + [jax.ShapeDtypeStruct(proj[0].shape, F32)] * 4,
-        input_output_aliases={1 + count + 6 + i: i for i in range(len(before))},
-    )(me, *blocks, *qkv, *proj, *before)
+            grid=(parts,),
+            in_specs=[
+                pl.BlockSpec((slab, size), functools.partial(lambda at, k, m: (0, at), at))
+                for at in places
+            ]
+            + [spec] * 3,
+            out_specs=[spec] * 4,
+            scratch_shapes=[pltpu.VMEM((slab, full), F32)],
+        ),
+        out_shape=[jax.ShapeDtypeStruct(weight.shape, F32)] * 4,
+    )(me, *blocks, weight, mean, second)
 
 
 def exchange(blocks, count):
@@ -624,8 +657,9 @@
 
 
 def attn_gradient_kernel(columns, me_ref, *refs):
-    shifted, grads, proj_ins, contexts, out = (refs[:2], refs[2:4], refs[4:6], refs[6:8], refs[8])
-    full = out.shape[1]
+    shifted, grads, proj_ins, contexts = (refs[:2], refs[2:4], refs[4:6], refs[6:8])
+    qkv_out, proj_out = refs[8:]
+    full = grads[0].shape[1]
     split = columns // 256 * 256
     for low, high in ((0, split), (split, full)):
         total = None
@@ -635,7 +669,12 @@
         for left, right in terms:
             part = dot_tn(left[...], right[:, low:high])
             total = part if total is None else total + part
-        out[:, low:high] = total.astype(BF16)
+        total = total.astype(BF16)
+        if high > columns:
+            qkv_out[:, low:] = total[:, : columns - low]
+            proj_out[...] = total[:, columns - low :]
+        else:
+            qkv_out[:, low:high] = total
 
 
 def attn_gradient(place, columns, shifted, grads, proj_ins, contexts):
@@ -651,9 +690,11 @@
             num_scalar_prefetch=1,
             grid=(width // tile,),
             in_specs=(left + right) * 2,
-            out_specs=pl.BlockSpec((tile, full), lambda i, m: (i, 0)),
-        ),
-        out_shape=jax.ShapeDtypeStruct((width, full), BF16),
+            out_specs=[
+                pl.BlockSpec((tile, size), lambda i, m: (i, 0)) for size in (columns, full - columns)
+            ],
+        ),
+        out_shape=[jax.ShapeDtypeStruct((width, size), BF16) for size in (columns, full - columns)],
         cost_estimate=pl.CostEstimate(
             flops=4 * rows * width * full, bytes_accessed=8 * rows * width, transcendentals=0
         ),
@@ -712,8 +753,9 @@
         return lax.all_gather(shard, "outer", axis=0, tiled=True)
 
     blocks = pack_attn(place, qkv_all[0], proj_all[0], count)
-    shard = unpack(place, exchange(blocks, count))
-    attn_both = full_weight(shard)
+    own_full = full_weight(blocks[0])
+    shard = jnp.concatenate(exchange(blocks, count)[1:], axis=0)
+    attn_both = merge(place, own_full, full_weight(shard), slab, count)
 
     half_width = width // 2
     frequency = jnp.exp(-math.log(10000.0) * jnp.arange(half_width, dtype=F32) / half_width)
@@ -849,7 +891,9 @@
                 place, 3 * head_cols, shifted_one[n], grad_qkv_rows[n], proj_ins[n], contexts[n]
             )
         )
-    attn_grad_sums = [outer_sum(grad_attn[n]) for n in streams]
+    qkv_sum = outer_sum(jnp.concatenate([pair[0] for pair in grad_attn], axis=1))
+    proj_both = jnp.concatenate([pair[1] for pair in grad_attn], axis=1)
+    proj_both = proj_both.reshape(-1, count, slab, proj_both.shape[1])
     grad_qkv_rows = after(grad_qkv_rows, grad_attn)
     partials = [[dot_nt(half, attn_full[n]) for half in grad_qkv_rows[n]] for n in streams]
     sent_one = send_both(partials, count)
@@ -877,6 +921,16 @@
         devices,
     )
 
+    blocks = exchange(
+        [
+            lax.dynamic_index_in_dim(proj_both, me ^ j, axis=1, keepdims=False)
+            for j in range(count)
+        ],
+        count,
+    )
+    blocks = after(blocks, to_owners)
+    proj_sum = outer_sum(jnp.concatenate(blocks, axis=2).reshape(-1, count * proj_both.shape[3]))
+
     received = lax.all_to_all(to_owners, every, split_axis=0, concat_axis=0, tiled=True)
     own_columns = received.reshape(seq_count, cores, 2, column_count).sum(axis=1)
     grad_mod = jnp.einsum(
@@ -895,22 +949,24 @@
     ff_sums[1] = after(ff_sums[1], to_owners)
     ff_outs = adam_both(1, ff_outs)
     down_outs, up_outs = ff_outs
-    attn_outs = adam_attn(
-        place, owned(after(attn_grad_sums[0], to_owners)), qkv_all, proj_all, 0, ()
-    )
-    last_sum = after(
-        attn_grad_sums[1], attn_outs[0], up_outs[0], down_outs[0], new_mod, text_out, text_grad
-    )
-    attn_outs = adam_attn(place, owned(last_sum), qkv_all, proj_all, 1, attn_outs)
+    qkv_outs = adam_attn(
+        place,
+        count,
+        owned(after(qkv_sum, new_mod, text_out, text_grad)),
+        *(a.reshape(6, *a.shape[2:]) for a in qkv_all),
+    )
+    proj_outs = adam_attn(
+        place, count, [after(proj_sum, qkv_outs[0], up_outs[0], down_outs[0])], *proj_all
+    )
     grad_up, new_up, mean_up_next, second_up_next = up_outs
     grad_down, new_down, mean_down_next, second_down_next = (
         a.transpose(0, 2, 1) for a in down_outs
     )
     grad_qkv, new_qkv, mean_qkv_next, second_qkv_next = (
-        a.transpose(0, 2, 1, 3) for a in attn_outs[:4]
+        a.reshape(qkv_all[0].shape).transpose(0, 2, 1, 3) for a in qkv_outs
     )
     grad_proj, new_proj, mean_proj_next, second_proj_next = (
-        a.transpose(0, 2, 1) for a in attn_outs[4:]
+        a.transpose(0, 2, 1) for a in proj_outs
     )
     return (
         image_out,

time: 663 us -> 663 us (level)
  waiting for transfers between devices: 231 us -> 202 us
  other arithmetic: 22.8 us -> 34.9 us
  blocking collectives: 0 us -> 11.2 us
    all_gather x3 -> x4, waiting for transfers between devices: 28 us -> 15 us  [full_weight(): return lax.all_gather(shard, 'outer', axis=0, tiled=True)]
    all_to_all x0 -> x1, blocking collectives: none -> 11.2 us  [local(): lax.all_to_all(to_owners, every, split_axis=0, concat_axis=0, tiled=True)]
    all_to_all x1, waiting for transfers between devices: 10.6 us -> 0.01 us  [local(): lax.all_to_all(to_cores, every, split_axis=0, concat_axis=0, tiled=True)]
    concatenate x0 -> x3, other arithmetic: none -> 9.42 us  [the longest x1 5.1 us: local(): jnp.concatenate([pair[0] for pair in grad_attn], axis=1)]
    pallas_call x2 -> x3, Pallas kernels: 10.4 us -> 15.7 us  [the longest x2 10.7 us: adam_attn(): pl.pallas_call(functools.partial(adam_attn_kernel, count, parts), grid_sp...]
    unnamed x244 -> x240, local copies, waits for them, and re-layouts: 24.4 us -> 28 us
  transfers between devices with their start and end apart: 86 -> 86, of which waited for: 36 -> 34; matrix products, arithmetic and copies ran while one was open for 28% -> 30% of each run, Pallas kernels for 18% -> 19%
where the time goes in v1:
time: 663 us; the launch traced here: 655 us
  waiting for transfers between devices  202 us (30%)
  Pallas kernels  130 us (20%)
  matrix products  121 us (18%)
  starting transfers between devices  82.5 us (12%)
  local copies, waits for them, and re-layouts  57.4 us (9%)
  other arithmetic  34.9 us (5%)
  between operations  16.2 us (2%)
  blocking collectives  11.2 us (2%)
    ppermute x60, waiting for transfers between devices, hop(): lax.ppermute(values, 'inner', [(i, i ^ distance) for i in range(count)])  172 us
    ppermute x60, starting transfers between devices, hop(): lax.ppermute(values, 'inner', [(i, i ^ distance) for i in range(count)])  73.8 us
    dot_general x16, matrix products, dot_nn(): lax.dot_general(a, b, (((1,), (0,)), ((), ())), preferred_element_type=F32)  43.6 us
    dot_general x16, matrix products, dot_nt(): lax.dot_general(a, b, (((1,), (1,)), ((), ())), preferred_element_type=F32)  43.3 us
    unnamed x240, local copies, waits for them, and re-layouts  28 us
    pallas_call x5, Pallas kernels, row_kernel(): pl.pallas_call(body, grid_spec=pltpu.PrefetchScalarGridSpec(num_scalar_pr...  26 us
    dot_general x8, matrix products, dot_tn(): lax.dot_general(a, b, (((0,), (0,)), ((), ())), preferred_element_type=F32)  21.7 us
    pallas_call x1, Pallas kernels, attend(): pl.pallas_call(functools.partial(attend_kernel, rows, heads, padded), gri...  20.6 us
  transfers between devices with their start and end apart: 86, of which 34 were waited for; matrix products, arithmetic and copies ran while one was open for 30% of the time, Pallas kernels for 19%

profile of v1, /device:TPU:0, one launch (start us, length us, event | category | flops | bytes accessed | tf_op | source)
XLA Modules:
  0.0 655.4 jit_solution(15767463956756399669)
XLA Ops:
  26.0 13.4 %collective-permute-done.1 = bf16[96,1536]{1,0:T(8,128)(2,1)} collective-permute-done((bf16[96,1536]{1,0:T(8,128)(2,1)}, bf16[96,1536]{1,0:T(8,128)(2,1)}, u32[]{:S(2)}, u32[]{:S(2)}) %collective-permute-start.1) | collective-permute-done | bytes 294944 | tf_op jit(solution)/shard_map/ppermute | solution.py:234
  47.1 14.7 %collective-permute-done.5 = bf16[208,1536]{1,0:T(8,128)(2,1)S(1)} collective-permute-done((bf16[208,1536]{1,0:T(8,128)(2,1)S(1)}, bf16[208,1536]{1,0:T(8,128)(2,1)S(1)}, u32[]{:S(2)}, u32[]{:S(2)}) %collective-permute-start.5) | collective-permute-done | bytes 639008 | tf_op jit(solution)/shard_map/ppermute | solution.py:234
  61.9 12.1 %collective-permute-done.4 = bf16[208,1536]{1,0:T(8,128)(2,1)S(1)} collective-permute-done((bf16[208,1536]{1,0:T(8,128)(2,1)S(1)}, bf16[208,1536]{1,0:T(8,128)(2,1)S(1)}, u32[]{:S(2)}, u32[]{:S(2)}) %collective-permute-start.4) | collective-permute-done | bytes 639008 | tf_op jit(solution)/shard_map/ppermute | solution.py:234
  89.1 6.1 collective-permute-done.8.refs_1_
  95.2 6.8 %collective-permute-done.9.refs_2_ = bf16[96,1536]{1,0:T(8,128)(2,1)} collective-permute-done((bf16[96,1536]{1,0:T(8,128)(2,1)}, bf16[96,1536]{1,0:T(8,128)(2,1)}, u32[]{:S(2)}, u32[]{:S(2)}) %collective-permute-start.9) | collective-permute-done | bytes 294944 | tf_op jit(solution)/shard_map/ppermute | solution.py:234
  104.6 12.2 %all-gather.7.cloned.1.call-done.others_ref = bf16[1152,1536]{1,0:T(8,128)(2,1)} async-done(((bf16[288,1536]{1,0:T(8,128)(2,1)}), bf16[1152,1536]{1,0:T(8,128)(2,1)}) %all-gather.7.cloned.1.call-update) | async-done | bytes 3538960 | tf_op jit(solution)/shard_map/all_gather | solution.py:753
  132.8 20.6 %attend.1 = (bf16[512,768]{1,0:T(8,128)(2,1)}, bf16[512,768]{1,0:T(8,128)(2,1)}, bf16[320,768]{1,0:T(8,128)(2,1)}, bf16[320,768]{1,0:T(8,128)(2,1)}, f32[4,416,128]{2,1,0:T(8,128)}) custom-call(s32[2]{0:T(128)} %pad_add_fusion.valid_ref, bf16[512,768]{1,0:T(8,128)(2,1)} %convolution_convert_fusion.5.refs_0_, ...), custom_call_target="tpu_custom_call" | custom-call | flops 531628032 | bytes 2555904 | tf_op jit(solution)/shard_map/attend/pallas_call | solution.py:177
  176.7 9.3 %collective-permute-done.14 = bf16[128,1536]{1,0:T(8,128)(2,1)S(1)} collective-permute-done((bf16[128,1536]{1,0:T(8,128)(2,1)}, bf16[128,1536]{1,0:T(8,128)(2,1)S(1)}, u32[]{:S(2)}, u32[]{:S(2)}) %collective-permute-start.14) | collective-permute-done | bytes 393248 | tf_op jit(solution)/shard_map/ppermute | solution.py:234
  186.0 19.9 %collective-permute-done.13 = bf16[128,1536]{1,0:T(8,128)(2,1)} collective-permute-done((bf16[128,1536]{1,0:T(8,128)(2,1)}, bf16[128,1536]{1,0:T(8,128)(2,1)}, u32[]{:S(2)}, u32[]{:S(2)}) %collective-permute-start.13) | collective-permute-done | bytes 393248 | tf_op jit(solution)/shard_map/ppermute | solution.py:234
  219.8 10.9 %collective-permute-done.19 = bf16[128,1536]{1,0:T(8,128)(2,1)S(1)} collective-permute-done((bf16[128,1536]{1,0:T(8,128)(2,1)S(1)}, bf16[128,1536]{1,0:T(8,128)(2,1)S(1)}, u32[]{:S(2)}, u32[]{:S(2)}) %collective-permute-start.19) | collective-permute-done | bytes 393248 | tf_op jit(solution)/shard_map/ppermute | solution.py:234
  294.9 6.4 collective-permute-done.25.refs_1_
  302.9 5.6 shard_map.442
  329.2 5.7 fusion.126
  390.3 6.6 %collective-permute-done.48 = bf16[80,1536]{1,0:T(8,128)(2,1)S(1)} collective-permute-done((bf16[80,1536]{1,0:T(8,128)(2,1)}, bf16[80,1536]{1,0:T(8,128)(2,1)S(1)}, u32[]{:S(2)}, u32[]{:S(2)}) %collective-permute-start.48) | collective-permute-done | bytes 245792 | tf_op jit(solution)/shard_map/ppermute | solution.py:234
  409.0 19.2 %attend_back.1 = (bf16[512,768]{1,0:T(8,128)(2,1)}, bf16[512,768]{1,0:T(8,128)(2,1)}, bf16[320,768]{1,0:T(8,128)(2,1)}, bf16[320,768]{1,0:T(8,128)(2,1)}) custom-call(s32[2]{0:T(128)} %pad_add_fusion.valid_ref, bf16[512,768]{1,0:T(8,128)(2,1)} %convolution_convert_fusion.5.refs_0_, bf16[512,768]{1,0:T(8,128)(2,1)} %convolution_convert_fusion.4.refs_1_, ...), custom_call_target="tpu_custom_call" | custom-call | flops 1329070080 | bytes 6389760 | tf_op jit(solution)/shard_map/attend_back/pallas_call | solution.py:203
  428.2 7.1 %shard_map.447 = (bf16[1536,576]{1,0:T(8,128)(2,1)}, bf16[1536,192]{1,0:T(8,128)(2,1)}) custom-call(s32[1]{0:T(128)} %bitcast.1.me_ref, bf16[320,1536]{1,0:T(8,128)(2,1)} %copy-done.14, bf16[320,1536]{1,0:T(8,128)(2,1)} %copy-done.43, bf16[320,768]{1,0:T(8,128)(2,1)} %get-tuple-element.209.refs_2_, bf16[320,768]{1,0:T(8,128)(2,1)} %get-tuple-element.208.refs_3_, ...), custom_call_target="tpu_custom_call" | custom-call | flops 1509949440 | bytes 3932160 | tf_op jit(solution)/shard_map/pallas_call | solution.py:687
  435.3 8.1 %shard_map.446 = (bf16[1536,576]{1,0:T(8,128)(2,1)}, bf16[1536,192]{1,0:T(8,128)(2,1)}) custom-call(s32[1]{0:T(128)} %bitcast.1.me_ref, bf16[512,1536]{1,0:T(8,128)(2,1)} %copy-done.7, bf16[512,1536]{1,0:T(8,128)(2,1)} %copy-done.21, bf16[512,768]{1,0:T(8,128)(2,1)} %get-tuple-element.206.refs_2_, bf16[512,768]{1,0:T(8,128)(2,1)} %get-tuple-element.207.refs_3_, ...), custom_call_target="tpu_custom_call" | custom-call | flops 2415919104 | bytes 6291456 | tf_op jit(solution)/shard_map/pallas_call | solution.py:687
  443.4 5.1 pad_maximum_fusion.2
  489.8 7.7 %collective-permute-done.52.refs_1_ = bf16[208,1536]{1,0:T(8,128)(2,1)} collective-permute-done((bf16[208,1536]{1,0:T(8,128)(2,1)}, bf16[208,1536]{1,0:T(8,128)(2,1)}, u32[]{:S(2)}, u32[]{:S(2)}) %collective-permute-start.52) | collective-permute-done | bytes 639008 | tf_op jit(solution)/shard_map/ppermute | solution.py:234
  502.3 9.5 %collective-permute-done.57.refs_3_ = bf16[208,1536]{1,0:T(8,128)(2,1)S(1)} collective-permute-done((bf16[208,1536]{1,0:T(8,128)(2,1)}, bf16[208,1536]{1,0:T(8,128)(2,1)S(1)}, u32[]{:S(2)}, u32[]{:S(2)}) %collective-permute-start.57) | collective-permute-done | bytes 639008 | tf_op jit(solution)/shard_map/ppermute | solution.py:234
  517.8 5.5 collective-permute-done.55.refs_3_
  524.1 5.7 collective-permute-done.54.refs_2_
  538.6 5.1 shard_map.449
  543.8 5.2 shard_map.448
  548.9 9.4 %shard_map.450 = (f32[208,1536]{1,0:T(8,128)}, f32[208,1536]{1,0:T(8,128)}, f32[32,2,288]{2,1,0:T(2,128)}) custom-call(s32[1]{0:T(128)} %bitcast.1.me_ref, f32[2,6,1536]{2,1,0:T(8,128)} %copy-done.19, bf16[208,1536]{1,0:T(8,128)(2,1)} %collective-permute-done.52.refs_1_, bf16[208,1536]{1,0:T(8,128)(2,1)} %collective-permute-done.56.refs_2_, ...), custom_call_target="tpu_custom_call" | custom-call | tf_op jit(solution)/shard_map/pallas_call | solution.py:510
  561.5 11.2 %all_to_all.10 = f32[32,2,288]{2,1,0:T(2,128)S(1)} all-to-all(f32[32,2,288]{2,1,0:T(2,128)S(1)} %copy-done.93), channel_id=1, replica_groups=mesh['outer'=4,'inner'=4,'tensor'=2] {'outer','inner','tensor'}, dimensions={0} | all-to-all | bytes 147456 | tf_op jit(solution)/shard_map/all_to_all | solution.py:934
  572.8 9.8 %multiply_subtract_fusion = (f32[2,1536,288]{1,2,0:T(8,128)}, f32[2,1536,288]{1,2,0:T(8,128)}, f32[2,1536,288]{1,2,0:T(8,128)}, f32[2,1536,288]{1,2,0:T(8,128)}) fusion(f32[2,1536,288]{1,2,0:T(8,128)} %param.28, f32[2,1536,288]{1,2,0:T(8,128)} %param.34, f32[2,1536,288]{1,2,0:T(8,128)} %param.35, f32[16,768]{1,0:T(8,128)S(1)} %copy-done.72, ...), kind=kOutput, calls=%fused_computation.9 | convolution fusion | flops 183287808 | bytes 24907776 | tf_op jit(solution)/shard_map/sd,snc->ndc/dot_general | solution.py:936
  594.2 8.1 %reduce-scatter.11.cloned.1.call-done = bf16[384,1536]{1,0:T(8,128)(2,1)} async-done(((bf16[1536,1536]{1,0:T(8,128)(2,1)}), bf16[384,1536]{1,0:T(8,128)(2,1)}) %reduce-scatter.11.cloned.1.call-update) | async-done | bytes 1179664 | tf_op jit(solution)/shard_map/reduce_scatter | solution.py:828
  616.6 8.5 %collective-permute-done.69.refs_2_ = bf16[96,1152]{1,0:T(8,128)(2,1)S(1)} collective-permute-done((bf16[96,1152]{1,0:T(8,128)(2,1)}, bf16[96,1152]{1,0:T(8,128)(2,1)S(1)}, u32[]{:S(2)}, u32[]{:S(2)}) %collective-permute-start.69) | collective-permute-done | bytes 221216 | tf_op jit(solution)/shard_map/ppermute | solution.py:234
  626.4 7.6 %shard_map.453 = (f32[6,96,768]{2,1,0:T(8,128)}, f32[6,96,768]{2,1,0:T(8,128)}, f32[6,96,768]{2,1,0:T(8,128)}, f32[6,96,768]{2,1,0:T(8,128)}) custom-call(s32[1]{0:T(128)} %bitcast.1.me_ref, bf16[96,1152]{1,0:T(8,128)(2,1)} %get-tuple-element.427.refs_0_, bf16[96,1152]{1,0:T(8,128)(2,1)} %copy-done.91, bf16[96,1152]{1,0:T(8,128)(2,1)} %copy-done.90, ...), custom_call_target="tpu_custom_call" | custom-call | tf_op jit(solution)/shard_map/pallas_call | solution.py:480
  635.0 5.1 shard_map.455
  640.1 5.2 shard_map.454
  (547 shorter events, 345.9 us)
Async XLA Ops:
  7.2 97.3 %all-gather.5.cloned.1.call-start = ((), (), s32[]{:S(2)}) async-start(), calls=%async_computation.6 | async-start | bytes 1474560 | tf_op jit(solution)/shard_map/all_gather | solution.py:753
  22.5 94.3 %all-gather.7.cloned.1.call-start = ((), (), s32[]{:S(2)}) async-start(), calls=%async_computation.7 | async-start | bytes 4423680 | tf_op jit(solution)/shard_map/all_gather | solution.py:753
  41.4 218.0 %all-gather.9.cloned.1.call-start = ((), (), s32[]{:S(2)}) async-start(), calls=%async_computation.8 | async-start | bytes 5898240 | tf_op jit(solution)/shard_map/all_gather | solution.py:753
  45.9 28.1 %collective-permute-start.4 = (bf16[208,1536]{1,0:T(8,128)(2,1)S(1)}, bf16[208,1536]{1,0:T(8,128)(2,1)S(1)}, u32[]{:S(2)}, u32[]{:S(2)}) collective-permute-start(bf16[208,1536]{1,0:T(8,128)(2,1)S(1)} %pad_maximum_fusion.12), channel_id=1, source_target_pairs={{0,4},{2,6},{4,0},{6,2},{1,5},{3,7},{5,1},{7,3},{8,12},{10,14},{12... | collective-permute-start | bytes 1916936 | tf_op jit(solution)/shard_map/ppermute | solution.py:234
  46.7 27.4 %collective-permute-start.3 = (bf16[208,1536]{1,0:T(8,128)(2,1)S(1)}, bf16[208,1536]{1,0:T(8,128)(2,1)S(1)}, u32[]{:S(2)}, u32[]{:S(2)}) collective-permute-start(bf16[208,1536]{1,0:T(8,128)(2,1)S(1)} %pad_maximum_fusion.12), channel_id=1, source_target_pairs={{0,2},{2,0},{4,6},{6,4},{1,3},{3,1},{5,7},{7,5},{8,10},{10,8},{12,... | collective-permute-start | bytes 1916936 | tf_op jit(solution)/shard_map/ppermute | solution.py:234
  104.3 233.4 %all-gather.11.cloned.1.call-start = ((), (), s32[]{:S(2)}) async-start(), calls=%async_computation.9 | async-start | bytes 5898240 | tf_op jit(solution)/shard_map/all_gather | solution.py:753
  167.3 38.6 %collective-permute-start.13 = (bf16[128,1536]{1,0:T(8,128)(2,1)}, bf16[128,1536]{1,0:T(8,128)(2,1)}, u32[]{:S(2)}, u32[]{:S(2)}) collective-permute-start(bf16[128,1536]{1,0:T(8,128)(2,1)} %get-tuple-element.399), channel_id=1, source_target_pairs={{0,4},{2,6},{4,0},{6,2},{1,5},{3,7},{5,1},{7,3},{8,12},{10,14},{12... | collective-permute-start | bytes 1179656 | tf_op jit(solution)/shard_map/ppermute | solution.py:234
  168.0 66.0 %collective-permute-start.17 = (bf16[208,1536]{1,0:T(8,128)(2,1)S(1)}, bf16[208,1536]{1,0:T(8,128)(2,1)}, u32[]{:S(2)}, u32[]{:S(2)}) collective-permute-start(bf16[208,1536]{1,0:T(8,128)(2,1)S(1)} %pad_maximum_fusion.13), channel_id=1, source_target_pairs={{0,6},{2,4},{4,2},{6,0},{1,7},{3,5},{5,3},{7,1},{8,14},{10,12},{12... | collective-permute-start | bytes 1916936 | tf_op jit(solution)/shard_map/ppermute | solution.py:234
  170.3 65.2 %collective-permute-start.16 = (bf16[208,1536]{1,0:T(8,128)(2,1)S(1)}, bf16[208,1536]{1,0:T(8,128)(2,1)}, u32[]{:S(2)}, u32[]{:S(2)}) collective-permute-start(bf16[208,1536]{1,0:T(8,128)(2,1)S(1)} %pad_maximum_fusion.13), channel_id=1, source_target_pairs={{0,4},{2,6},{4,0},{6,2},{1,5},{3,7},{5,1},{7,3},{8,12},{10,14},{12... | collective-permute-start | bytes 1916936 | tf_op jit(solution)/shard_map/ppermute | solution.py:234
  176.7 35.4 %collective-permute-start.31 = (bf16[320,1536]{1,0:T(8,128)(2,1)S(1)}, bf16[320,1536]{1,0:T(8,128)(2,1)S(1)}, u32[]{:S(2)}, u32[]{:S(2)}) collective-permute-start(bf16[320,1536]{1,0:T(8,128)(2,1)S(1)} %convolution_convert_fusion.1), channel_id=1, source_target_pairs={{0,1},{1,0},{2,3},{3,2},{4,5},{5,4},{6,7},{7,6},{8,9},{9,8},{10,11... | collective-permute-start | bytes 2949128 | tf_op jit(solution)/shard_map/ppermute | solution.py:230
  250.2 233.2 %reduce-scatter.5.cloned.1.call-start = ((), (), s32[]{:S(2)}) async-start(), calls=%async_computation.10 | async-start | bytes 5898240 | tf_op jit(solution)/shard_map/reduce_scatter | solution.py:828
  268.7 44.4 %collective-permute-start.37 = (bf16[80,1536]{1,0:T(8,128)(2,1)S(1)}, bf16[80,1536]{1,0:T(8,128)(2,1)}, u32[]{:S(2)}, u32[]{:S(2)}) collective-permute-start(bf16[80,1536]{1,0:T(8,128)(2,1)S(1)} %add_convert_fusion.5), channel_id=1, source_target_pairs={{0,6},{2,4},{4,2},{6,0},{1,7},{3,5},{5,3},{7,1},{8,14},{10,12},{12... | collective-permute-start | bytes 737288 | tf_op jit(solution)/shard_map/ppermute | solution.py:234
  270.7 42.4 %collective-permute-start.36 = (bf16[80,1536]{1,0:T(8,128)(2,1)S(1)}, bf16[80,1536]{1,0:T(8,128)(2,1)}, u32[]{:S(2)}, u32[]{:S(2)}) collective-permute-start(bf16[80,1536]{1,0:T(8,128)(2,1)S(1)} %add_convert_fusion.5), channel_id=1, source_target_pairs={{0,4},{2,6},{4,0},{6,2},{1,5},{3,7},{5,1},{7,3},{8,12},{10,14},{12... | collective-permute-start | bytes 737288 | tf_op jit(solution)/shard_map/ppermute | solution.py:234
  315.3 27.0 %collective-permute-start.42 = (bf16[320,1536]{1,0:T(8,128)(2,1)}, bf16[320,1536]{1,0:T(8,128)(2,1)}, u32[]{:S(2)}, u32[]{:S(2)}) collective-permute-start(bf16[320,1536]{1,0:T(8,128)(2,1)} %pad_maximum_fusion.11), channel_id=1, source_target_pairs={{0,1},{1,0},{2,3},{3,2},{4,5},{5,4},{6,7},{7,6},{8,9},{9,8},{10,11... | collective-permute-start | bytes 2949128 | tf_op jit(solution)/shard_map/ppermute | solution.py:230
  323.8 266.8 %reduce-scatter.7.cloned.1.call-start = ((), (), s32[]{:S(2)}) async-start(), calls=%async_computation.11 | async-start | bytes 4423680 | tf_op jit(solution)/shard_map/reduce_scatter | solution.py:828
  323.8 32.0 %collective-permute-start.29 = (bf16[128,1536]{1,0:T(8,128)(2,1)}, bf16[128,1536]{1,0:T(8,128)(2,1)}, u32[]{:S(2)}, u32[]{:S(2)}) collective-permute-start(bf16[128,1536]{1,0:T(8,128)(2,1)} %get-tuple-element.175), channel_id=1, source_target_pairs={{0,6},{2,4},{4,2},{6,0},{1,7},{3,5},{5,3},{7,1},{8,14},{10,12},{12... | collective-permute-start | bytes 1179656 | tf_op jit(solution)/shard_map/ppermute | solution.py:234
  324.9 29.1 %collective-permute-start.28 = (bf16[128,1536]{1,0:T(8,128)(2,1)}, bf16[128,1536]{1,0:T(8,128)(2,1)}, u32[]{:S(2)}, u32[]{:S(2)}) collective-permute-start(bf16[128,1536]{1,0:T(8,128)(2,1)} %get-tuple-element.175), channel_id=1, source_target_pairs={{0,4},{2,6},{4,0},{6,2},{1,5},{3,7},{5,1},{7,3},{8,12},{10,14},{12... | collective-permute-start | bytes 1179656 | tf_op jit(solution)/shard_map/ppermute | solution.py:234
  357.6 44.3 %collective-permute-start.30 = (bf16[512,1536]{1,0:T(8,128)(2,1)}, bf16[512,1536]{1,0:T(8,128)(2,1)}, u32[]{:S(2)}, u32[]{:S(2)}) collective-permute-start(bf16[512,1536]{1,0:T(8,128)(2,1)} %constant_dynamic-update-slice_fusion.3.refs_4_), channel_id=1, source_target_pairs={{0,1},{1,0},{2,3},{3,2},{4,5},{5,4},{6,7},{7,6},{8,9},{9,8},{10,11... | collective-permute-start | bytes 4718600 | tf_op jit(solution)/shard_map/ppermute | solution.py:230
  448.5 153.9 %reduce-scatter.11.cloned.1.call-start = ((), (), s32[]{:S(2)}) async-start(), calls=%async_computation.13 | async-start | bytes 5898240 | tf_op jit(solution)/shard_map/reduce_scatter | solution.py:828
  452.7 192.5 %reduce-scatter.9.cloned.1.call-start = ((), (), s32[]{:S(2)}) async-start(), calls=%async_computation.12 | async-start | bytes 1474560 | tf_op jit(solution)/shard_map/reduce_scatter | solution.py:828
  483.5 28.3 %collective-permute-start.57 = (bf16[208,1536]{1,0:T(8,128)(2,1)}, bf16[208,1536]{1,0:T(8,128)(2,1)S(1)}, u32[]{:S(2)}, u32[]{:S(2)}) collective-permute-start(bf16[208,1536]{1,0:T(8,128)(2,1)} %pad_maximum_fusion.16), channel_id=1, source_target_pairs={{0,6},{2,4},{4,2},{6,0},{1,7},{3,5},{5,3},{7,1},{8,14},{10,12},{12... | collective-permute-start | bytes 1916936 | tf_op jit(solution)/shard_map/ppermute | solution.py:234
  486.8 30.2 %collective-permute-start.65 = (bf16[80,1536]{1,0:T(8,128)(2,1)}, bf16[80,1536]{1,0:T(8,128)(2,1)S(1)}, u32[]{:S(2)}, u32[]{:S(2)}) collective-permute-start(bf16[80,1536]{1,0:T(8,128)(2,1)} %get-tuple-element.412), channel_id=1, source_target_pairs={{0,6},{2,4},{4,2},{6,0},{1,7},{3,5},{5,3},{7,1},{8,14},{10,12},{12... | collective-permute-start | bytes 737288 | tf_op jit(solution)/shard_map/ppermute | solution.py:234
  488.4 34.9 %collective-permute-start.55 = (bf16[96,1536]{1,0:T(8,128)(2,1)S(1)}, bf16[96,1536]{1,0:T(8,128)(2,1)S(1)}, u32[]{:S(2)}, u32[]{:S(2)}) collective-permute-start(bf16[96,1536]{1,0:T(8,128)(2,1)S(1)} %get-tuple-element.408), channel_id=1, source_target_pairs={{0,6},{2,4},{4,2},{6,0},{1,7},{3,5},{5,3},{7,1},{8,14},{10,12},{12... | collective-permute-start | bytes 884744 | tf_op jit(solution)/shard_map/ppermute | solution.py:234
  497.4 32.3 %collective-permute-start.54 = (bf16[96,1536]{1,0:T(8,128)(2,1)S(1)}, bf16[96,1536]{1,0:T(8,128)(2,1)S(1)}, u32[]{:S(2)}, u32[]{:S(2)}) collective-permute-start(bf16[96,1536]{1,0:T(8,128)(2,1)S(1)} %get-tuple-element.409), channel_id=1, source_target_pairs={{0,4},{2,6},{4,0},{6,2},{1,5},{3,7},{5,1},{7,3},{8,12},{10,14},{12... | collective-permute-start | bytes 884744 | tf_op jit(solution)/shard_map/ppermute | solution.py:234
  498.7 31.8 %collective-permute-start.53 = (bf16[96,1536]{1,0:T(8,128)(2,1)S(1)}, bf16[96,1536]{1,0:T(8,128)(2,1)S(1)}, u32[]{:S(2)}, u32[]{:S(2)}) collective-permute-start(bf16[96,1536]{1,0:T(8,128)(2,1)S(1)} %get-tuple-element.410), channel_id=1, source_target_pairs={{0,2},{2,0},{4,6},{6,4},{1,3},{3,1},{5,7},{7,5},{8,10},{10,8},{12,... | collective-permute-start | bytes 884744 | tf_op jit(solution)/shard_map/ppermute | solution.py:234
  511.8 46.5 %collective-permute-start.73 = (bf16[4,96,384]{2,1,0:T(8,128)(2,1)}, bf16[4,96,384]{2,1,0:T(8,128)(2,1)}, u32[]{:S(2)}, u32[]{:S(2)}) collective-permute-start(bf16[4,96,384]{2,1,0:T(8,128)(2,1)} %get-tuple-element.405), channel_id=1, source_target_pairs={{0,6},{2,4},{4,2},{6,0},{1,7},{3,5},{5,3},{7,1},{8,14},{10,12},{12... | collective-permute-start | bytes 884744 | tf_op jit(solution)/shard_map/ppermute | solution.py:234
  517.1 41.3 %collective-permute-start.72 = (bf16[4,96,384]{2,1,0:T(8,128)(2,1)}, bf16[4,96,384]{2,1,0:T(8,128)(2,1)}, u32[]{:S(2)}, u32[]{:S(2)}) collective-permute-start(bf16[4,96,384]{2,1,0:T(8,128)(2,1)} %get-tuple-element.406), channel_id=1, source_target_pairs={{0,4},{2,6},{4,0},{6,2},{1,5},{3,7},{5,1},{7,3},{8,12},{10,14},{12... | collective-permute-start | bytes 884744 | tf_op jit(solution)/shard_map/ppermute | solution.py:234
  523.3 35.0 %collective-permute-start.71 = (bf16[4,96,384]{2,1,0:T(8,128)(2,1)}, bf16[4,96,384]{2,1,0:T(8,128)(2,1)}, u32[]{:S(2)}, u32[]{:S(2)}) collective-permute-start(bf16[4,96,384]{2,1,0:T(8,128)(2,1)} %get-tuple-element.407), channel_id=1, source_target_pairs={{0,2},{2,0},{4,6},{6,4},{1,3},{3,1},{5,7},{7,5},{8,10},{10,8},{12,... | collective-permute-start | bytes 884744 | tf_op jit(solution)/shard_map/ppermute | solution.py:234
  561.0 26.2 %collective-permute-start.67 = (f32[208,1536]{1,0:T(8,128)S(1)}, f32[208,1536]{1,0:T(8,128)}, u32[]{:S(2)}, u32[]{:S(2)}) collective-permute-start(f32[208,1536]{1,0:T(8,128)S(1)} %copy-done.33), channel_id=1, source_target_pairs={{0,1},{1,0},{2,3},{3,2},{4,5},{5,4},{6,7},{7,6},{8,9},{9,8},{10,11... | collective-permute-start | bytes 3833864 | tf_op jit(solution)/shard_map/ppermute | solution.py:230
  604.4 29.7 %collective-permute-start.76 = (bf16[96,1536]{1,0:T(8,128)(2,1)S(1)}, bf16[96,1536]{1,0:T(8,128)(2,1)S(1)}, u32[]{:S(2)}, u32[]{:S(2)}) collective-permute-start(bf16[96,1536]{1,0:T(8,128)(2,1)S(1)} %get-tuple-element.400), channel_id=1, source_target_pairs={{0,6},{2,4},{4,2},{6,0},{1,7},{3,5},{5,3},{7,1},{8,14},{10,12},{12... | collective-permute-start | bytes 884744 | tf_op jit(solution)/shard_map/ppermute | solution.py:234
  606.8 27.3 %collective-permute-start.75 = (bf16[96,1536]{1,0:T(8,128)(2,1)S(1)}, bf16[96,1536]{1,0:T(8,128)(2,1)S(1)}, u32[]{:S(2)}, u32[]{:S(2)}) collective-permute-start(bf16[96,1536]{1,0:T(8,128)(2,1)S(1)} %get-tuple-element.401), channel_id=1, source_target_pairs={{0,4},{2,6},{4,0},{6,2},{1,5},{3,7},{5,1},{7,3},{8,12},{10,14},{12... | collective-permute-start | bytes 884744 | tf_op jit(solution)/shard_map/ppermute | solution.py:234
  607.3 26.8 %collective-permute-start.74 = (bf16[96,1536]{1,0:T(8,128)(2,1)S(1)}, bf16[96,1536]{1,0:T(8,128)(2,1)S(1)}, u32[]{:S(2)}, u32[]{:S(2)}) collective-permute-start(bf16[96,1536]{1,0:T(8,128)(2,1)S(1)} %get-tuple-element.402), channel_id=1, source_target_pairs={{0,2},{2,0},{4,6},{6,4},{1,3},{3,1},{5,7},{7,5},{8,10},{10,8},{12,... | collective-permute-start | bytes 884744 | tf_op jit(solution)/shard_map/ppermute | solution.py:234
  (169 other events, 2342.8 us)
Sparse Core Ops, SparseCore 0:
  10.4 35.3 all-gather.4
  48.0 68.7 all-gather.6
  118.9 87.9 all-gather.8
  250.4 87.2 all-gather.10
  339.8 83.6 reduce-scatter.4
  448.6 64.3 reduce-scatter.6
  515.3 87.0 reduce-scatter.10
  604.7 29.7 reduce-scatter.8

commit v2 on v1

--- a/solution.py
+++ b/solution.py
@@ -909,14 +909,13 @@
         ]
 
     ff_outs = adam_both(0, ((), ()))
+    sent_one = after(sent_one, down_partials, ff_outs[0][0], ff_outs[1][0])
+    ff_sums[1] = after(ff_sums[1], sent_one[1], [sent[1] for sent in down_sent])
     grad_rows, out_rows, to_owners = end_rows(
         place,
         mods,
-        after(sent_one, down_partials, ff_outs[0][0], ff_outs[1][0]),
-        [
-            (tokens[n], grad_middles[n], cotangents[n], middles[n], partial_rows[n])
-            for n in streams
-        ],
+        sent_one,
+        [(tokens[n], grad_middles[n], cotangents[n], middles[n], partial_rows[n]) for n in streams],
         down_sent,
         devices,
     )
@@ -932,6 +931,8 @@
     proj_sum = outer_sum(jnp.concatenate(blocks, axis=2).reshape(-1, count * proj_both.shape[3]))
 
     received = lax.all_to_all(to_owners, every, split_axis=0, concat_axis=0, tiled=True)
+    ff_outs = adam_both(1, ff_outs)
+    received = after(received, ff_outs[0][0], ff_outs[1][0])
     own_columns = received.reshape(seq_count, cores, 2, column_count).sum(axis=1)
     grad_mod = jnp.einsum(
         "sd,snc->ndc", all_cond.astype(F32), own_columns, precision=lax.Precision.HIGHEST
@@ -946,8 +947,6 @@
     image_out, text_out = whole_rows(core_place, out_rows, lengths)
     image_grad, text_grad = whole_rows(core_place, grad_rows, lengths)
 
-    ff_sums[1] = after(ff_sums[1], to_owners)
-    ff_outs = adam_both(1, ff_outs)
     down_outs, up_outs = ff_outs
     qkv_outs = adam_attn(
         place,

time: 663 us -> 679 us (1.024)
  waiting for transfers between devices: 202 us -> 240 us
  blocking collectives: 11.2 us -> 0 us
  other arithmetic: 34.9 us -> 26.1 us
    ppermute x60, waiting for transfers between devices: 172 us -> 221 us  [hop(): lax.ppermute(values, 'inner', [(i, i ^ distance) for i in range(count)])]
    all_to_all x1 -> x0, blocking collectives: 11.2 us -> none  [local(): lax.all_to_all(to_owners, every, split_axis=0, concat_axis=0, tiled=True)]
    reduce_scatter x4, waiting for transfers between devices: 8.17 us -> 0.04 us  [outer_sum(): return lax.psum_scatter(gradient, 'outer', scatter_dimension=0, tiled=True)]
    unnamed x240 -> x250, local copies, waits for them, and re-layouts: 28 us -> 28.5 us
  transfers between devices with their start and end apart: 86 -> 87, of which waited for: 34 -> 38; matrix products, arithmetic and copies ran while one was open for 30% -> 27% of each run, Pallas kernels for 19% -> 19%
where the time goes in v2:
time: 679 us; the launch traced here: 672 us
  waiting for transfers between devices  240 us (35%)
  Pallas kernels  131 us (19%)
  matrix products  115 us (17%)
  starting transfers between devices  87.3 us (13%)
  local copies, waits for them, and re-layouts  57.3 us (8%)
  other arithmetic  26.1 us (4%)
  between operations  16.2 us (2%)
    ppermute x60, waiting for transfers between devices, hop(): lax.ppermute(values, 'inner', [(i, i ^ distance) for i in range(count)])  221 us
    ppermute x60, starting transfers between devices, hop(): lax.ppermute(values, 'inner', [(i, i ^ distance) for i in range(count)])  76.1 us
    dot_general x16, matrix products, dot_nt(): lax.dot_general(a, b, (((1,), (1,)), ((), ())), preferred_element_type=F32)  43.1 us
    dot_general x16, matrix products, dot_nn(): lax.dot_general(a, b, (((1,), (0,)), ((), ())), preferred_element_type=F32)  42.6 us
    unnamed x250, local copies, waits for them, and re-layouts  28.5 us
    pallas_call x5, Pallas kernels, row_kernel(): pl.pallas_call(body, grid_spec=pltpu.PrefetchScalarGridSpec(num_scalar_pr...  26 us
    pallas_call x1, Pallas kernels, attend(): pl.pallas_call(functools.partial(attend_kernel, rows, heads, padded), gri...  20.7 us
    pallas_call x4, Pallas kernels, adam_ff(): pl.pallas_call(functools.partial(adam_ff_kernel, count), grid_spec=pltpu....  20.4 us
  transfers between devices with their start and end apart: 87, of which 38 were waited for; matrix products, arithmetic and copies ran while one was open for 27% of the time, Pallas kernels for 19%

profile of v2, /device:TPU:0, one launch (start us, length us, event | category | flops | bytes accessed | tf_op | source)
XLA Modules:
  0.0 672.2 jit_solution(10441872022437118182)
XLA Ops:
  26.0 13.4 %collective-permute-done.1 = bf16[96,1536]{1,0:T(8,128)(2,1)} collective-permute-done((bf16[96,1536]{1,0:T(8,128)(2,1)}, bf16[96,1536]{1,0:T(8,128)(2,1)}, u32[]{:S(2)}, u32[]{:S(2)}) %collective-permute-start.1) | collective-permute-done | bytes 294944 | tf_op jit(solution)/shard_map/ppermute | solution.py:234
  47.1 14.7 %collective-permute-done.5 = bf16[208,1536]{1,0:T(8,128)(2,1)S(1)} collective-permute-done((bf16[208,1536]{1,0:T(8,128)(2,1)S(1)}, bf16[208,1536]{1,0:T(8,128)(2,1)S(1)}, u32[]{:S(2)}, u32[]{:S(2)}) %collective-permute-start.5) | collective-permute-done | bytes 639008 | tf_op jit(solution)/shard_map/ppermute | solution.py:234
  61.9 12.1 %collective-permute-done.4 = bf16[208,1536]{1,0:T(8,128)(2,1)S(1)} collective-permute-done((bf16[208,1536]{1,0:T(8,128)(2,1)S(1)}, bf16[208,1536]{1,0:T(8,128)(2,1)S(1)}, u32[]{:S(2)}, u32[]{:S(2)}) %collective-permute-start.4) | collective-permute-done | bytes 639008 | tf_op jit(solution)/shard_map/ppermute | solution.py:234
  89.1 6.1 collective-permute-done.8.refs_1_
  95.2 6.8 %collective-permute-done.9.refs_2_ = bf16[96,1536]{1,0:T(8,128)(2,1)} collective-permute-done((bf16[96,1536]{1,0:T(8,128)(2,1)}, bf16[96,1536]{1,0:T(8,128)(2,1)}, u32[]{:S(2)}, u32[]{:S(2)}) %collective-permute-start.9) | collective-permute-done | bytes 294944 | tf_op jit(solution)/shard_map/ppermute | solution.py:234
  104.6 12.2 %all-gather.7.cloned.1.call-done.others_ref = bf16[1152,1536]{1,0:T(8,128)(2,1)} async-done(((bf16[288,1536]{1,0:T(8,128)(2,1)}), bf16[1152,1536]{1,0:T(8,128)(2,1)}) %all-gather.7.cloned.1.call-update) | async-done | bytes 3538960 | tf_op jit(solution)/shard_map/all_gather | solution.py:753
  132.5 20.7 %attend.1 = (bf16[512,768]{1,0:T(8,128)(2,1)}, bf16[512,768]{1,0:T(8,128)(2,1)}, bf16[320,768]{1,0:T(8,128)(2,1)}, bf16[320,768]{1,0:T(8,128)(2,1)}, f32[4,416,128]{2,1,0:T(8,128)}) custom-call(s32[2]{0:T(128)} %pad_add_fusion.valid_ref, bf16[512,768]{1,0:T(8,128)(2,1)} %convolution_convert_fusion.5.refs_0_, ...), custom_call_target="tpu_custom_call" | custom-call | flops 531628032 | bytes 2555904 | tf_op jit(solution)/shard_map/attend/pallas_call | solution.py:177
  165.4 8.4 %collective-permute-done.12 = bf16[128,1536]{1,0:T(8,128)(2,1)S(1)} collective-permute-done((bf16[128,1536]{1,0:T(8,128)(2,1)S(1)}, bf16[128,1536]{1,0:T(8,128)(2,1)S(1)}, u32[]{:S(2)}, u32[]{:S(2)}) %collective-permute-start.12) | collective-permute-done | bytes 393248 | tf_op jit(solution)/shard_map/ppermute | solution.py:234
  173.8 8.4 %collective-permute-done.14 = bf16[128,1536]{1,0:T(8,128)(2,1)S(1)} collective-permute-done((bf16[128,1536]{1,0:T(8,128)(2,1)S(1)}, bf16[128,1536]{1,0:T(8,128)(2,1)S(1)}, u32[]{:S(2)}, u32[]{:S(2)}) %collective-permute-start.14) | collective-permute-done | bytes 393248 | tf_op jit(solution)/shard_map/ppermute | solution.py:234
  192.0 6.2 collective-permute-done.20
  199.7 7.0 %collective-permute-done.19 = bf16[128,1536]{1,0:T(8,128)(2,1)S(1)} collective-permute-done((bf16[128,1536]{1,0:T(8,128)(2,1)S(1)}, bf16[128,1536]{1,0:T(8,128)(2,1)S(1)}, u32[]{:S(2)}, u32[]{:S(2)}) %collective-permute-start.19) | collective-permute-done | bytes 393248 | tf_op jit(solution)/shard_map/ppermute | solution.py:234
  212.4 8.0 %collective-permute-done.17 = bf16[208,1536]{1,0:T(8,128)(2,1)S(1)} collective-permute-done((bf16[208,1536]{1,0:T(8,128)(2,1)S(1)}, bf16[208,1536]{1,0:T(8,128)(2,1)S(1)}, u32[]{:S(2)}, u32[]{:S(2)}) %collective-permute-start.17) | collective-permute-done | bytes 639008 | tf_op jit(solution)/shard_map/ppermute | solution.py:234
  221.1 10.0 %collective-permute-done.16 = bf16[208,1536]{1,0:T(8,128)(2,1)S(1)} collective-permute-done((bf16[208,1536]{1,0:T(8,128)(2,1)S(1)}, bf16[208,1536]{1,0:T(8,128)(2,1)S(1)}, u32[]{:S(2)}, u32[]{:S(2)}) %collective-permute-start.16) | collective-permute-done | bytes 639008 | tf_op jit(solution)/shard_map/ppermute | solution.py:234
  235.8 8.1 %collective-permute-done.40.refs_3_ = bf16[96,1536]{1,0:T(8,128)(2,1)} collective-permute-done((bf16[96,1536]{1,0:T(8,128)(2,1)}, bf16[96,1536]{1,0:T(8,128)(2,1)}, u32[]{:S(2)}, u32[]{:S(2)}) %collective-permute-start.40) | collective-permute-done | bytes 294944 | tf_op jit(solution)/shard_map/ppermute | solution.py:234
  295.5 10.4 %collective-permute-done.33 = bf16[80,1536]{1,0:T(8,128)(2,1)S(1)} collective-permute-done((bf16[80,1536]{1,0:T(8,128)(2,1)S(1)}, bf16[80,1536]{1,0:T(8,128)(2,1)S(1)}, u32[]{:S(2)}, u32[]{:S(2)}) %collective-permute-start.33) | collective-permute-done | bytes 245792 | tf_op jit(solution)/shard_map/ppermute | solution.py:234
  313.6 5.6 shard_map.442
  326.3 6.3 collective-permute-done.37
  378.9 7.7 %collective-permute-done.27 = bf16[128,1536]{1,0:T(8,128)(2,1)S(1)} collective-permute-done((bf16[128,1536]{1,0:T(8,128)(2,1)S(1)}, bf16[128,1536]{1,0:T(8,128)(2,1)S(1)}, u32[]{:S(2)}, u32[]{:S(2)}) %collective-permute-start.27) | collective-permute-done | bytes 393248 | tf_op jit(solution)/shard_map/ppermute | solution.py:234
  387.4 9.5 %collective-permute-done.28 = bf16[128,1536]{1,0:T(8,128)(2,1)S(1)} collective-permute-done((bf16[128,1536]{1,0:T(8,128)(2,1)S(1)}, bf16[128,1536]{1,0:T(8,128)(2,1)S(1)}, u32[]{:S(2)}, u32[]{:S(2)}) %collective-permute-start.28) | collective-permute-done | bytes 393248 | tf_op jit(solution)/shard_map/ppermute | solution.py:234
  425.0 5.7 collective-permute-done.48
  442.9 19.2 %attend_back.1 = (bf16[512,768]{1,0:T(8,128)(2,1)}, bf16[512,768]{1,0:T(8,128)(2,1)}, bf16[320,768]{1,0:T(8,128)(2,1)}, bf16[320,768]{1,0:T(8,128)(2,1)}) custom-call(s32[2]{0:T(128)} %pad_add_fusion.valid_ref, bf16[512,768]{1,0:T(8,128)(2,1)} %convolution_convert_fusion.5.refs_0_, bf16[512,768]{1,0:T(8,128)(2,1)} %convolution_convert_fusion.4.refs_1_, ...), custom_call_target="tpu_custom_call" | custom-call | flops 1329070080 | bytes 6389760 | tf_op jit(solution)/shard_map/attend_back/pallas_call | solution.py:203
  462.1 7.2 %shard_map.447 = (bf16[1536,576]{1,0:T(8,128)(2,1)}, bf16[1536,192]{1,0:T(8,128)(2,1)}) custom-call(s32[1]{0:T(128)} %bitcast.1.me_ref, bf16[320,1536]{1,0:T(8,128)(2,1)} %copy-done.15, bf16[320,1536]{1,0:T(8,128)(2,1)} %copy-done.46, bf16[320,768]{1,0:T(8,128)(2,1)} %get-tuple-element.210.refs_2_, bf16[320,768]{1,0:T(8,128)(2,1)} %get-tuple-element.209.refs_3_, ...), custom_call_target="tpu_custom_call" | custom-call | flops 1509949440 | bytes 3932160 | tf_op jit(solution)/shard_map/pallas_call | solution.py:687
  469.3 8.3 %shard_map.446 = (bf16[1536,576]{1,0:T(8,128)(2,1)}, bf16[1536,192]{1,0:T(8,128)(2,1)}) custom-call(s32[1]{0:T(128)} %bitcast.1.me_ref, bf16[512,1536]{1,0:T(8,128)(2,1)} %copy-done.7, bf16[512,1536]{1,0:T(8,128)(2,1)} %copy-done.30, bf16[512,768]{1,0:T(8,128)(2,1)} %get-tuple-element.207.refs_2_, bf16[512,768]{1,0:T(8,128)(2,1)} %get-tuple-element.208.refs_3_, ...), custom_call_target="tpu_custom_call" | custom-call | flops 2415919104 | bytes 6291456 | tf_op jit(solution)/shard_map/pallas_call | solution.py:687
  497.1 5.3 fusion.127
  516.9 8.8 %collective-permute-done.52.refs_1_ = bf16[208,1536]{1,0:T(8,128)(2,1)} collective-permute-done((bf16[208,1536]{1,0:T(8,128)(2,1)}, bf16[208,1536]{1,0:T(8,128)(2,1)}, u32[]{:S(2)}, u32[]{:S(2)}) %collective-permute-start.52) | collective-permute-done | bytes 639008 | tf_op jit(solution)/shard_map/ppermute | solution.py:234
  528.6 10.9 %collective-permute-done.57.refs_3_ = bf16[208,1536]{1,0:T(8,128)(2,1)} collective-permute-done((bf16[208,1536]{1,0:T(8,128)(2,1)S(1)}, bf16[208,1536]{1,0:T(8,128)(2,1)}, u32[]{:S(2)}, u32[]{:S(2)}) %collective-permute-start.57) | collective-permute-done | bytes 639008 | tf_op jit(solution)/shard_map/ppermute | solution.py:234
  549.6 6.7 collective-permute-done.55.refs_3_
  571.4 5.1 shard_map.449
  581.6 9.3 %shard_map.450 = (f32[208,1536]{1,0:T(8,128)}, f32[208,1536]{1,0:T(8,128)}, f32[32,2,288]{2,1,0:T(2,128)}) custom-call(s32[1]{0:T(128)} %bitcast.1.me_ref, f32[2,6,1536]{2,1,0:T(8,128)} %copy-done.23, bf16[208,1536]{1,0:T(8,128)(2,1)} %collective-permute-done.52.refs_1_, bf16[208,1536]{1,0:T(8,128)(2,1)} %copy-done.69, ...), custom_call_target="tpu_custom_call" | custom-call | tf_op jit(solution)/shard_map/pallas_call | solution.py:510
  628.6 9.8 %multiply_subtract_fusion = (f32[2,1536,288]{1,2,0:T(8,128)}, f32[2,1536,288]{1,2,0:T(8,128)}, f32[2,1536,288]{1,2,0:T(8,128)}, f32[2,1536,288]{1,2,0:T(8,128)}) fusion(f32[2,1536,288]{1,2,0:T(8,128)} %param.28, f32[2,1536,288]{1,2,0:T(8,128)} %param.34, f32[2,1536,288]{1,2,0:T(8,128)} %param.35, f32[16,768]{1,0:T(8,128)S(1)} %copy-done.80, ...), kind=kOutput, calls=%fused_computation.9 | convolution fusion | flops 183287808 | bytes 24907776 | tf_op jit(solution)/shard_map/sd,snc->ndc/dot_general | solution.py:937
  644.5 5.1 collective-permute-done.73.refs_3_
  654.5 7.6 %shard_map.455 = (f32[6,96,768]{2,1,0:T(8,128)}, f32[6,96,768]{2,1,0:T(8,128)}, f32[6,96,768]{2,1,0:T(8,128)}, f32[6,96,768]{2,1,0:T(8,128)}) custom-call(s32[1]{0:T(128)} %bitcast.1.me_ref, bf16[96,1152]{1,0:T(8,128)(2,1)} %get-tuple-element.429.refs_0_, bf16[96,1152]{1,0:T(8,128)(2,1)} %copy-done.98, bf16[96,1152]{1,0:T(8,128)(2,1)} %copy-done.97, ...), custom_call_target="tpu_custom_call" | custom-call | tf_op jit(solution)/shard_map/pallas_call | solution.py:480
  (557 shorter events, 365.3 us)
Async XLA Ops:
  7.2 97.3 %all-gather.5.cloned.1.call-start = ((), (), s32[]{:S(2)}) async-start(), calls=%async_computation.6 | async-start | bytes 1474560 | tf_op jit(solution)/shard_map/all_gather | solution.py:753
  17.6 24.5 %all-to-all-start = ((f32[32,2,288]{2,1,0:T(2,128)}), f32[32,2,288]{2,1,0:T(2,128)S(1)}, u32[]{:S(2)}, u32[]{:S(2)}) async-start(f32[32,2,288]{2,1,0:T(2,128)} %bitcast.3), calls=%async_computation | async-start | bytes 196608 | tf_op jit(solution)/shard_map/all_to_all | solution.py:772
  22.5 94.3 %all-gather.7.cloned.1.call-start = ((), (), s32[]{:S(2)}) async-start(), calls=%async_computation.7 | async-start | bytes 4423680 | tf_op jit(solution)/shard_map/all_gather | solution.py:753
  41.4 205.3 %all-gather.9.cloned.1.call-start = ((), (), s32[]{:S(2)}) async-start(), calls=%async_computation.8 | async-start | bytes 5898240 | tf_op jit(solution)/shard_map/all_gather | solution.py:753
  45.9 28.1 %collective-permute-start.4 = (bf16[208,1536]{1,0:T(8,128)(2,1)S(1)}, bf16[208,1536]{1,0:T(8,128)(2,1)S(1)}, u32[]{:S(2)}, u32[]{:S(2)}) collective-permute-start(bf16[208,1536]{1,0:T(8,128)(2,1)S(1)} %pad_maximum_fusion.12), channel_id=1, source_target_pairs={{0,4},{2,6},{4,0},{6,2},{1,5},{3,7},{5,1},{7,3},{8,12},{10,14},{12... | collective-permute-start | bytes 1916936 | tf_op jit(solution)/shard_map/ppermute | solution.py:234
  46.7 27.4 %collective-permute-start.3 = (bf16[208,1536]{1,0:T(8,128)(2,1)S(1)}, bf16[208,1536]{1,0:T(8,128)(2,1)S(1)}, u32[]{:S(2)}, u32[]{:S(2)}) collective-permute-start(bf16[208,1536]{1,0:T(8,128)(2,1)S(1)} %pad_maximum_fusion.12), channel_id=1, source_target_pairs={{0,2},{2,0},{4,6},{6,4},{1,3},{3,1},{5,7},{7,5},{8,10},{10,8},{12,... | collective-permute-start | bytes 1916936 | tf_op jit(solution)/shard_map/ppermute | solution.py:234
  104.3 245.4 %all-gather.11.cloned.1.call-start = ((), (), s32[]{:S(2)}) async-start(), calls=%async_computation.9 | async-start | bytes 5898240 | tf_op jit(solution)/shard_map/all_gather | solution.py:753
  189.0 31.4 %collective-permute-start.17 = (bf16[208,1536]{1,0:T(8,128)(2,1)S(1)}, bf16[208,1536]{1,0:T(8,128)(2,1)S(1)}, u32[]{:S(2)}, u32[]{:S(2)}) collective-permute-start(bf16[208,1536]{1,0:T(8,128)(2,1)S(1)} %pad_maximum_fusion.13), channel_id=1, source_target_pairs={{0,6},{2,4},{4,2},{6,0},{1,7},{3,5},{5,3},{7,1},{8,14},{10,12},{12... | collective-permute-start | bytes 1916936 | tf_op jit(solution)/shard_map/ppermute | solution.py:234
  190.5 40.6 %collective-permute-start.16 = (bf16[208,1536]{1,0:T(8,128)(2,1)S(1)}, bf16[208,1536]{1,0:T(8,128)(2,1)S(1)}, u32[]{:S(2)}, u32[]{:S(2)}) collective-permute-start(bf16[208,1536]{1,0:T(8,128)(2,1)S(1)} %pad_maximum_fusion.13), channel_id=1, source_target_pairs={{0,4},{2,6},{4,0},{6,2},{1,5},{3,7},{5,1},{7,3},{8,12},{10,14},{12... | collective-permute-start | bytes 1916936 | tf_op jit(solution)/shard_map/ppermute | solution.py:234
  198.2 35.2 %collective-permute-start.15 = (bf16[208,1536]{1,0:T(8,128)(2,1)S(1)}, bf16[208,1536]{1,0:T(8,128)(2,1)}, u32[]{:S(2)}, u32[]{:S(2)}) collective-permute-start(bf16[208,1536]{1,0:T(8,128)(2,1)S(1)} %pad_maximum_fusion.13), channel_id=1, source_target_pairs={{0,2},{2,0},{4,6},{6,4},{1,3},{3,1},{5,7},{7,5},{8,10},{10,8},{12,... | collective-permute-start | bytes 1916936 | tf_op jit(solution)/shard_map/ppermute | solution.py:234
  208.1 38.6 %collective-permute-start.22 = (bf16[512,1536]{1,0:T(8,128)(2,1)}, bf16[512,1536]{1,0:T(8,128)(2,1)}, u32[]{:S(2)}, u32[]{:S(2)}) collective-permute-start(bf16[512,1536]{1,0:T(8,128)(2,1)} %pad_maximum_fusion.6), channel_id=1, source_target_pairs={{0,1},{1,0},{2,3},{3,2},{4,5},{5,4},{6,7},{7,6},{8,9},{9,8},{10,11... | collective-permute-start | bytes 4718600 | tf_op jit(solution)/shard_map/ppermute | solution.py:230
  210.9 32.9 %collective-permute-start.38 = (bf16[96,1536]{1,0:T(8,128)(2,1)}, bf16[96,1536]{1,0:T(8,128)(2,1)}, u32[]{:S(2)}, u32[]{:S(2)}) collective-permute-start(bf16[96,1536]{1,0:T(8,128)(2,1)} %get-tuple-element.180), channel_id=1, source_target_pairs={{0,2},{2,0},{4,6},{6,4},{1,3},{3,1},{5,7},{7,5},{8,10},{10,8},{12,... | collective-permute-start | bytes 884744 | tf_op jit(solution)/shard_map/ppermute | solution.py:234
  220.4 23.5 %collective-permute-start.39 = (bf16[96,1536]{1,0:T(8,128)(2,1)}, bf16[96,1536]{1,0:T(8,128)(2,1)}, u32[]{:S(2)}, u32[]{:S(2)}) collective-permute-start(bf16[96,1536]{1,0:T(8,128)(2,1)} %get-tuple-element.182), channel_id=1, source_target_pairs={{0,4},{2,6},{4,0},{6,2},{1,5},{3,7},{5,1},{7,3},{8,12},{10,14},{12... | collective-permute-start | bytes 884744 | tf_op jit(solution)/shard_map/ppermute | solution.py:234
  246.2 265.8 %reduce-scatter.5.cloned.1.call-start = ((), (), s32[]{:S(2)}) async-start(), calls=%async_computation.10 | async-start | bytes 5898240 | tf_op jit(solution)/shard_map/reduce_scatter | solution.py:828
  277.5 316.4 %reduce-scatter.7.cloned.1.call-start = ((), (), s32[]{:S(2)}) async-start(), calls=%async_computation.11 | async-start | bytes 5898240 | tf_op jit(solution)/shard_map/reduce_scatter | solution.py:828
  285.1 24.1 %collective-permute-start.26 = (bf16[128,1536]{1,0:T(8,128)(2,1)S(1)}, bf16[128,1536]{1,0:T(8,128)(2,1)S(1)}, u32[]{:S(2)}, u32[]{:S(2)}) collective-permute-start(bf16[128,1536]{1,0:T(8,128)(2,1)S(1)} %get-tuple-element.396), channel_id=1, source_target_pairs={{0,6},{2,4},{4,2},{6,0},{1,7},{3,5},{5,3},{7,1},{8,14},{10,12},{12... | collective-permute-start | bytes 1179656 | tf_op jit(solution)/shard_map/ppermute | solution.py:234
  286.2 26.5 %collective-permute-start.25 = (bf16[128,1536]{1,0:T(8,128)(2,1)S(1)}, bf16[128,1536]{1,0:T(8,128)(2,1)S(1)}, u32[]{:S(2)}, u32[]{:S(2)}) collective-permute-start(bf16[128,1536]{1,0:T(8,128)(2,1)S(1)} %get-tuple-element.397), channel_id=1, source_target_pairs={{0,4},{2,6},{4,0},{6,2},{1,5},{3,7},{5,1},{7,3},{8,12},{10,14},{12... | collective-permute-start | bytes 1179656 | tf_op jit(solution)/shard_map/ppermute | solution.py:234
  322.3 22.7 %collective-permute-start.58 = (bf16[512,1536]{1,0:T(8,128)(2,1)S(1)}, bf16[512,1536]{1,0:T(8,128)(2,1)S(1)}, u32[]{:S(2)}, u32[]{:S(2)}) collective-permute-start(bf16[512,1536]{1,0:T(8,128)(2,1)S(1)} %fusion.41), channel_id=1, source_target_pairs={{0,1},{1,0},{2,3},{3,2},{4,5},{5,4},{6,7},{7,6},{8,9},{9,8},{10,11... | collective-permute-start | bytes 4718600 | tf_op jit(solution)/shard_map/ppermute | solution.py:230
  373.7 264.7 %reduce-scatter.9.cloned.1.call-start = ((), (), s32[]{:S(2)}) async-start(), calls=%async_computation.12 | async-start | bytes 4423680 | tf_op jit(solution)/shard_map/reduce_scatter | solution.py:828
  376.0 25.4 %collective-permute-start.29 = (bf16[128,1536]{1,0:T(8,128)(2,1)S(1)}, bf16[128,1536]{1,0:T(8,128)(2,1)S(1)}, u32[]{:S(2)}, u32[]{:S(2)}) collective-permute-start(bf16[128,1536]{1,0:T(8,128)(2,1)S(1)} %copy-done.90), channel_id=1, source_target_pairs={{0,6},{2,4},{4,2},{6,0},{1,7},{3,5},{5,3},{7,1},{8,14},{10,12},{12... | collective-permute-start | bytes 1179656 | tf_op jit(solution)/shard_map/ppermute | solution.py:234
  402.1 33.6 %collective-permute-start.30 = (bf16[512,1536]{1,0:T(8,128)(2,1)}, bf16[512,1536]{1,0:T(8,128)(2,1)}, u32[]{:S(2)}, u32[]{:S(2)}) collective-permute-start(bf16[512,1536]{1,0:T(8,128)(2,1)} %constant_dynamic-update-slice_fusion.3.refs_4_), channel_id=1, source_target_pairs={{0,1},{1,0},{2,3},{3,2},{4,5},{5,4},{6,7},{7,6},{8,9},{9,8},{10,11... | collective-permute-start | bytes 4718600 | tf_op jit(solution)/shard_map/ppermute | solution.py:230
  489.5 172.6 %reduce-scatter.11.cloned.1.call-start = ((), (), s32[]{:S(2)}) async-start(), calls=%async_computation.13 | async-start | bytes 1474560 | tf_op jit(solution)/shard_map/reduce_scatter | solution.py:828
  510.1 29.4 %collective-permute-start.57 = (bf16[208,1536]{1,0:T(8,128)(2,1)S(1)}, bf16[208,1536]{1,0:T(8,128)(2,1)}, u32[]{:S(2)}, u32[]{:S(2)}) collective-permute-start(bf16[208,1536]{1,0:T(8,128)(2,1)S(1)} %pad_maximum_fusion.16), channel_id=1, source_target_pairs={{0,6},{2,4},{4,2},{6,0},{1,7},{3,5},{5,3},{7,1},{8,14},{10,12},{12... | collective-permute-start | bytes 1916936 | tf_op jit(solution)/shard_map/ppermute | solution.py:234
  512.1 32.5 %collective-permute-start.65 = (bf16[80,1536]{1,0:T(8,128)(2,1)}, bf16[80,1536]{1,0:T(8,128)(2,1)S(1)}, u32[]{:S(2)}, u32[]{:S(2)}) collective-permute-start(bf16[80,1536]{1,0:T(8,128)(2,1)} %get-tuple-element.414), channel_id=1, source_target_pairs={{0,6},{2,4},{4,2},{6,0},{1,7},{3,5},{5,3},{7,1},{8,14},{10,12},{12... | collective-permute-start | bytes 737288 | tf_op jit(solution)/shard_map/ppermute | solution.py:234
  515.9 65.7 %collective-permute-start.64 = (bf16[80,1536]{1,0:T(8,128)(2,1)}, bf16[80,1536]{1,0:T(8,128)(2,1)}, u32[]{:S(2)}, u32[]{:S(2)}) collective-permute-start(bf16[80,1536]{1,0:T(8,128)(2,1)} %get-tuple-element.415), channel_id=1, source_target_pairs={{0,4},{2,6},{4,0},{6,2},{1,5},{3,7},{5,1},{7,3},{8,12},{10,14},{12... | collective-permute-start | bytes 737288 | tf_op jit(solution)/shard_map/ppermute | solution.py:234
  525.8 55.9 %collective-permute-start.63 = (bf16[80,1536]{1,0:T(8,128)(2,1)}, bf16[80,1536]{1,0:T(8,128)(2,1)}, u32[]{:S(2)}, u32[]{:S(2)}) collective-permute-start(bf16[80,1536]{1,0:T(8,128)(2,1)} %get-tuple-element.416), channel_id=1, source_target_pairs={{0,2},{2,0},{4,6},{6,4},{1,3},{3,1},{5,7},{7,5},{8,10},{10,8},{12,... | collective-permute-start | bytes 737288 | tf_op jit(solution)/shard_map/ppermute | solution.py:234
  527.3 28.9 %collective-permute-start.55 = (bf16[96,1536]{1,0:T(8,128)(2,1)S(1)}, bf16[96,1536]{1,0:T(8,128)(2,1)S(1)}, u32[]{:S(2)}, u32[]{:S(2)}) collective-permute-start(bf16[96,1536]{1,0:T(8,128)(2,1)S(1)} %get-tuple-element.410), channel_id=1, source_target_pairs={{0,6},{2,4},{4,2},{6,0},{1,7},{3,5},{5,3},{7,1},{8,14},{10,12},{12... | collective-permute-start | bytes 884744 | tf_op jit(solution)/shard_map/ppermute | solution.py:234
  539.5 22.8 %collective-permute-start.54 = (bf16[96,1536]{1,0:T(8,128)(2,1)S(1)}, bf16[96,1536]{1,0:T(8,128)(2,1)S(1)}, u32[]{:S(2)}, u32[]{:S(2)}) collective-permute-start(bf16[96,1536]{1,0:T(8,128)(2,1)S(1)} %get-tuple-element.411), channel_id=1, source_target_pairs={{0,4},{2,6},{4,0},{6,2},{1,5},{3,7},{5,1},{7,3},{8,12},{10,14},{12... | collective-permute-start | bytes 884744 | tf_op jit(solution)/shard_map/ppermute | solution.py:234
  556.2 35.3 %collective-permute-start.76 = (bf16[4,96,384]{2,1,0:T(8,128)(2,1)}, bf16[4,96,384]{2,1,0:T(8,128)(2,1)}, u32[]{:S(2)}, u32[]{:S(2)}) collective-permute-start(bf16[4,96,384]{2,1,0:T(8,128)(2,1)} %get-tuple-element.403), channel_id=1, source_target_pairs={{0,6},{2,4},{4,2},{6,0},{1,7},{3,5},{5,3},{7,1},{8,14},{10,12},{12... | collective-permute-start | bytes 884744 | tf_op jit(solution)/shard_map/ppermute | solution.py:234
  562.3 29.2 %collective-permute-start.75 = (bf16[4,96,384]{2,1,0:T(8,128)(2,1)}, bf16[4,96,384]{2,1,0:T(8,128)(2,1)}, u32[]{:S(2)}, u32[]{:S(2)}) collective-permute-start(bf16[4,96,384]{2,1,0:T(8,128)(2,1)} %get-tuple-element.404), channel_id=1, source_target_pairs={{0,4},{2,6},{4,0},{6,2},{1,5},{3,7},{5,1},{7,3},{8,12},{10,14},{12... | collective-permute-start | bytes 884744 | tf_op jit(solution)/shard_map/ppermute | solution.py:234
  563.8 27.7 %collective-permute-start.74 = (bf16[4,96,384]{2,1,0:T(8,128)(2,1)}, bf16[4,96,384]{2,1,0:T(8,128)(2,1)}, u32[]{:S(2)}, u32[]{:S(2)}) collective-permute-start(bf16[4,96,384]{2,1,0:T(8,128)(2,1)} %get-tuple-element.405), channel_id=1, source_target_pairs={{0,2},{2,0},{4,6},{6,4},{1,3},{3,1},{5,7},{7,5},{8,10},{10,8},{12,... | collective-permute-start | bytes 884744 | tf_op jit(solution)/shard_map/ppermute | solution.py:234
  599.6 28.8 %all-to-all-start.1 = ((f32[32,2,288]{2,1,0:T(2,128)}), f32[32,2,288]{2,1,0:T(2,128)S(1)}, u32[]{:S(2)}, u32[]{:S(2)}) async-start(f32[32,2,288]{2,1,0:T(2,128)} %get-tuple-element.235), calls=%async_computation.2 | async-start | bytes 196608 | tf_op jit(solution)/shard_map/all_to_all | solution.py:933
  (175 other events, 1876.5 us)
Sparse Core Ops, SparseCore 0:
  10.4 35.3 all-gather.4
  48.0 68.7 all-gather.6
  118.9 87.9 all-gather.8
  246.4 86.5 all-gather.10
  335.1 83.6 reduce-scatter.4
  421.0 85.7 reduce-scatter.6
  509.2 66.9 reduce-scatter.8
  594.0 27.9 reduce-scatter.10
